TPU v7x, 32 devices: a whole 2x2x4 slice. The times are simulated.
32 devices in a mesh: dp: 4 (over z), expert: 8 (over y, x, core).
Axes of the slice: x: 2, y: 2, z: 4, core: 2. Of those that a mesh axis runs over, the one named last changes fastest.
Arguments:
- tokens: bfloat16 [8192, 768], P(('dp', 'expert')), may hold values from -6 to 6
- segment_ids: int32 [32, 256], P(('dp', 'expert')), may hold values from 0 to 2, never falling along the last dimension, each value on 1 to 204 neighbouring positions
- routes: int32 [8192, 2], P(('dp', 'expert')), may hold values from 0 to 15, all different within a row
- ln1_gain: float32 [768], P('dp'), may hold values from 0.5 to 1.5
- ln1_bias: float32 [768], P('dp'), may hold values from -0.6 to 0.6
- ln2_gain: float32 [768], P('dp'), may hold values from 0.5 to 1.5
- ln2_bias: float32 [768], P('dp'), may hold values from -0.6 to 0.6
- w_query: float32 [768, 768], P('dp'), may hold values from -0.3125 to 0.3125
- w_key: float32 [768, 768], P('dp'), may hold values from -0.3125 to 0.3125
- w_value: float32 [768, 768], P('dp'), may hold values from -0.21875 to 0.21875
- w_output: float32 [768, 768], P('dp'), may hold values from -0.875 to 0.875
- w_router: float32 [768, 16], P('dp'), may hold values from -0.15625 to 0.15625
- frozen_in: float32 [8, 768, 3072], P('expert', 'dp'), may hold values from -0.21875 to 0.21875
- frozen_out: float32 [8, 3072, 768], P('expert', 'dp'), may hold values from -0.1875 to 0.1875
- new_in: float32 [8, 768, 3072], P('expert', 'dp'), may hold values from -0.21875 to 0.21875
- new_out: float32 [8, 3072, 768], P('expert', 'dp'), may hold values from -0.1875 to 0.1875
- cotangent: bfloat16 [8192, 768], P(('dp', 'expert')), may hold values from -6 to 6
Outputs:
- block_out: bfloat16 [8192, 768], P(('dp', 'expert'))
- grad_tokens: bfloat16 [8192, 768], P(('dp', 'expert'))
- grad_w_query: float32 [768, 768], P('dp')
- grad_w_key: float32 [768, 768], P('dp')
- grad_w_value: float32 [768, 768], P('dp')
- grad_w_output: float32 [768, 768], P('dp')
- grad_w_router: float32 [768, 16], P('dp')
- grad_ln1_gain: float32 [768], P('dp')
- grad_ln1_bias: float32 [768], P('dp')
- grad_ln2_gain: float32 [768], P('dp')
- grad_ln2_bias: float32 [768], P('dp')
- grad_new_in: float32 [8, 768, 3072], P('expert', 'dp')
- grad_new_out: float32 [8, 3072, 768], P('expert', 'dp')
Inputs may be any that keep to these rules, and one draw needn't show every extreme that they name: `segment_ids`: within each row ids never fall, every sequence has 1 to 204 tokens, and one has exactly 204. `routes`: the two experts of a token differ.
All inputs are finite; a program needn't handle non-finite values.
Results may differ from a plain program's by a relative error of at most 0.014.
The roundings to bfloat16 on the way count: a program that leaves them out, or rounds other values in their place, can miss the bound.
Values may be sent and summed in bfloat16 or wider, within the bound.
A program may use at most 192 MiB of HBM per device.

v0:
```python
import jax
import jax.numpy as jnp
from jax import lax
from jax.sharding import PartitionSpec as P

HEADS = 12
HEAD = 64


NORM_EPS = 1e-05
MASKED = -1e30


def layer_norm(values, norm_gain, norm_shift):
    average = jnp.mean(values, axis=-1, keepdims=True)
    centred = values - average
    variance = jnp.mean(centred * centred, axis=-1, keepdims=True)
    return centred * lax.rsqrt(variance + NORM_EPS) * norm_gain + norm_shift


def inner_rows(left, right):
    return lax.dot_general(
        left, right, (((0,), (0,)), ((), ())), preferred_element_type=jnp.float32
    )


def times_transposed(left, right):
    return lax.dot_general(
        left, right, (((1,), (1,)), ((), ())), preferred_element_type=jnp.float32
    )


def shards(
    tokens,
    segment_ids,
    routes,
    ln1_gain,
    ln1_bias,
    ln2_gain,
    ln2_bias,
    w_query,
    w_key,
    w_value,
    w_output,
    w_router,
    frozen_in,
    frozen_out,
    new_in,
    new_out,
    cotangent,
):
    row_count = tokens.shape[0]
    model_width = tokens.shape[1]
    expert_count = w_router.shape[1]
    owner_count = expert_count // 2
    capacity = 5 * row_count // (2 * expert_count)
    slot_count = expert_count * capacity
    score_scale = HEAD ** (-0.5)
    (
        full_query,
        full_key,
        full_value,
        full_output,
        full_router,
        gain_one,
        bias_one,
        gain_two,
        bias_two,
    ) = (
        lax.all_gather(w_query.astype(jnp.bfloat16), "dp", axis=0, tiled=True),
        lax.all_gather(w_key.astype(jnp.bfloat16), "dp", axis=0, tiled=True),
        lax.all_gather(w_value.astype(jnp.bfloat16), "dp", axis=0, tiled=True),
        lax.all_gather(w_output.astype(jnp.bfloat16), "dp", axis=0, tiled=True),
        lax.all_gather(w_router.astype(jnp.bfloat16), "dp", axis=0, tiled=True),
        lax.all_gather(ln1_gain.astype(jnp.bfloat16), "dp", axis=0, tiled=True),
        lax.all_gather(ln1_bias.astype(jnp.bfloat16), "dp", axis=0, tiled=True),
        lax.all_gather(ln2_gain.astype(jnp.bfloat16), "dp", axis=0, tiled=True),
        lax.all_gather(ln2_bias.astype(jnp.bfloat16), "dp", axis=0, tiled=True),
    )
    full_frozen_in, full_frozen_out, full_new_in, full_new_out = (
        lax.all_gather(frozen_in[0].astype(jnp.bfloat16), "dp", axis=0, tiled=True),
        lax.all_gather(frozen_out[0].astype(jnp.bfloat16), "dp", axis=0, tiled=True),
        lax.all_gather(new_in[0].astype(jnp.bfloat16), "dp", axis=0, tiled=True),
        lax.all_gather(new_out[0].astype(jnp.bfloat16), "dp", axis=0, tiled=True),
    )
    stack_in = jnp.stack([full_frozen_in, full_new_in])
    stack_out = jnp.stack([full_frozen_out, full_new_out])
    gain_one_f = gain_one.astype(jnp.float32)
    bias_one_f = bias_one.astype(jnp.float32)
    gain_two_f = gain_two.astype(jnp.float32)
    bias_two_f = bias_two.astype(jnp.float32)
    rows_float = tokens.astype(jnp.float32)
    act_one = layer_norm(rows_float, gain_one_f, bias_one_f).astype(jnp.bfloat16)
    query_rows = jnp.dot(act_one, full_query, preferred_element_type=jnp.float32).astype(
        jnp.bfloat16
    )
    key_rows = jnp.dot(act_one, full_key, preferred_element_type=jnp.float32).astype(jnp.bfloat16)
    value_rows = jnp.dot(act_one, full_value, preferred_element_type=jnp.float32).astype(
        jnp.bfloat16
    )
    query_heads = query_rows.reshape(row_count, HEADS, HEAD)
    key_heads = key_rows.reshape(row_count, HEADS, HEAD)
    value_heads = value_rows.reshape(row_count, HEADS, HEAD)
    segments = segment_ids[0]
    positions = jnp.arange(row_count, dtype=jnp.int32)

    def block_scores(block_index):
        lower = block_index * row_count
        upper_end = lower + row_count
        scores = (
            jnp.einsum("qhd,khd->hqk", query_heads, key_heads, preferred_element_type=jnp.float32)
            * score_scale
        )
        allowed = (segments[lower:upper_end, None] == segments[None, :upper_end]) & (
            positions[None, :upper_end] <= positions[lower:upper_end, None]
        )
        return (jnp.where(allowed[None], scores, MASKED), allowed)

    block_index = 0
    upper_end = (block_index + 1) * row_count
    scores, allowed = block_scores(block_index)
    row_max = jnp.max(scores, axis=-1, keepdims=True)
    expo = jnp.exp(scores - row_max)
    row_total = jnp.sum(expo, axis=-1, keepdims=True)
    probabilities = expo / row_total
    log_totals = [row_max + jnp.log(row_total)]
    attended_parts = jnp.einsum(
        "hqk,khd->qhd",
        probabilities.astype(jnp.bfloat16),
        value_heads,
        preferred_element_type=jnp.float32,
    )
    attended = attended_parts.reshape(row_count, model_width).astype(jnp.bfloat16)
    residual = rows_float + jnp.dot(attended, full_output, preferred_element_type=jnp.float32)
    normed_two = layer_norm(residual, gain_two_f, bias_two_f)
    act_two = normed_two.astype(jnp.bfloat16)
    logits = jnp.dot(act_two, full_router, preferred_element_type=jnp.float32)
    expert_iota = jnp.arange(expert_count, dtype=jnp.int32)
    choose = (routes[:, :, None] == expert_iota[None, None, :]).astype(jnp.float32)
    picked = jnp.sum(choose * logits[:, None, :], axis=2)
    gate_values = jax.nn.softmax(picked, axis=-1)
    flat_ids = routes.reshape(2 * row_count)
    onehot = (flat_ids[:, None] == expert_iota[None, :]).astype(jnp.int32)
    running = jnp.cumsum(onehot, axis=0)
    position = jnp.sum(onehot * running, axis=1) - 1
    is_kept = position < capacity
    kept_float = is_kept.astype(jnp.float32)
    slot_index = (flat_ids % owner_count * 2 + flat_ids // owner_count) * capacity + position
    safe_slot = jnp.where(is_kept, slot_index, 0)
    pair_iota = jnp.arange(2 * row_count, dtype=jnp.int32)
    pair_of_slot = (
        jnp.full((slot_count + 1,), 2 * row_count, jnp.int32)
        .at[jnp.where(is_kept, slot_index, slot_count)]
        .set(pair_iota)[:slot_count]
    )
    token_of_slot = pair_of_slot // 2
    padded_act = jnp.concatenate([act_two, jnp.zeros((1, model_width), jnp.bfloat16)], axis=0)
    dispatched = padded_act[token_of_slot].reshape(owner_count, 2, capacity, model_width)
    received_rows = lax.all_to_all(dispatched, "expert", split_axis=0, concat_axis=0, tiled=True)
    pre_values = jnp.einsum(
        "sekd,edf->sekf", received_rows, stack_in, preferred_element_type=jnp.float32
    )
    hidden = jax.nn.gelu(pre_values).astype(jnp.bfloat16)
    produced_rows = jnp.einsum(
        "sekf,efd->sekd", hidden, stack_out, preferred_element_type=jnp.float32
    ).astype(jnp.bfloat16)
    returned = lax.all_to_all(
        produced_rows, "expert", split_axis=0, concat_axis=0, tiled=True
    ).reshape(slot_count, model_width)
    pair_out = returned[safe_slot].astype(jnp.float32)
    pair_weight = gate_values.reshape(2 * row_count) * kept_float
    mixture = jnp.sum((pair_out * pair_weight[:, None]).reshape(row_count, 2, model_width), axis=1)
    block_out = (residual + mixture).astype(jnp.bfloat16)
    d_out = cotangent.astype(jnp.float32)
    d_out_pairs = jnp.repeat(d_out, 2, axis=0)
    d_gate = kept_float * jnp.sum(pair_out * d_out_pairs, axis=1)
    slot_weight = jnp.concatenate([pair_weight, jnp.zeros((1,), jnp.float32)])[pair_of_slot]
    padded_grad = jnp.concatenate([d_out, jnp.zeros((1, model_width), jnp.float32)], axis=0)
    d_send = (
        (padded_grad[token_of_slot] * slot_weight[:, None])
        .astype(jnp.bfloat16)
        .reshape(owner_count, 2, capacity, model_width)
    )
    again_frozen_in, again_frozen_out, again_new_in, again_new_out = (
        lax.all_gather(frozen_in[0].astype(jnp.bfloat16), "dp", axis=0, tiled=True),
        lax.all_gather(frozen_out[0].astype(jnp.bfloat16), "dp", axis=0, tiled=True),
        lax.all_gather(new_in[0].astype(jnp.bfloat16), "dp", axis=0, tiled=True),
        lax.all_gather(new_out[0].astype(jnp.bfloat16), "dp", axis=0, tiled=True),
    )
    back_in = jnp.stack([again_frozen_in, again_new_in])
    back_out = jnp.stack([again_frozen_out, again_new_out])
    d_produced = lax.all_to_all(d_send, "expert", split_axis=0, concat_axis=0, tiled=True)
    d_hidden = jnp.einsum(
        "sekd,efd->sekf", d_produced, back_out, preferred_element_type=jnp.float32
    )
    gelu_value, gelu_back = jax.vjp(jax.nn.gelu, pre_values)
    d_pre = gelu_back(d_hidden)[0].astype(jnp.bfloat16)
    hidden_again = gelu_value.astype(jnp.bfloat16)
    d_received = jnp.einsum(
        "sekf,edf->sekd", d_pre, back_in, preferred_element_type=jnp.float32
    ).astype(jnp.bfloat16)
    grad_in_full = jnp.einsum(
        "skd,skf->df", received_rows[:, 1], d_pre[:, 1], preferred_element_type=jnp.float32
    )
    grad_out_full = jnp.einsum(
        "skf,skd->fd", hidden_again[:, 1], d_produced[:, 1], preferred_element_type=jnp.float32
    )
    grad_in_part, grad_out_part = (
        lax.psum_scatter(
            grad_in_full.astype(jnp.bfloat16), "dp", scatter_dimension=0, tiled=True
        ).astype(jnp.float32),
        lax.psum_scatter(
            grad_out_full.astype(jnp.bfloat16), "dp", scatter_dimension=0, tiled=True
        ).astype(jnp.float32),
    )
    d_returned = lax.all_to_all(
        d_received, "expert", split_axis=0, concat_axis=0, tiled=True
    ).reshape(slot_count, model_width)
    d_act_moe = jnp.sum(
        (d_returned[safe_slot].astype(jnp.float32) * kept_float[:, None]).reshape(
            row_count, 2, model_width
        ),
        axis=1,
    )
    d_gate_rows = d_gate.reshape(row_count, 2)
    d_picked = gate_values * (
        d_gate_rows - jnp.sum(gate_values * d_gate_rows, axis=1, keepdims=True)
    )
    d_logits = jnp.sum(choose * d_picked[:, :, None], axis=1).astype(jnp.bfloat16)
    grad_router = inner_rows(act_two, d_logits)
    d_act_two = d_act_moe + times_transposed(d_logits, full_router)
    norm_two_value, norm_two_back = jax.vjp(layer_norm, residual, gain_two_f, bias_two_f)
    d_resid_norm, grad_gain_two, grad_bias_two = norm_two_back(d_act_two)
    d_residual = d_out + d_resid_norm
    d_branch = d_residual.astype(jnp.bfloat16)
    grad_output = inner_rows(attended, d_branch)
    d_attended = (
        times_transposed(d_branch, full_output).astype(jnp.bfloat16).reshape(row_count, HEADS, HEAD)
    )
    block_index = 0
    lower = block_index * row_count
    upper_end = lower + row_count
    scores, allowed = block_scores(block_index)
    probabilities = jnp.exp(scores - log_totals[block_index])
    grad_probs = jnp.einsum(
        "qhd,khd->hqk", d_attended, value_heads, preferred_element_type=jnp.float32
    )
    row_delta = jnp.sum(grad_probs * probabilities, axis=-1, keepdims=True)
    grad_scores = jnp.where(allowed[None], probabilities * (grad_probs - row_delta), 0.0).astype(
        jnp.bfloat16
    )
    d_query_parts = (
        jnp.einsum("hqk,khd->qhd", grad_scores, key_heads, preferred_element_type=jnp.float32)
        * score_scale
    )
    d_key_sum = (
        jnp.einsum("hqk,qhd->khd", grad_scores, query_heads, preferred_element_type=jnp.float32)
        * score_scale
    )
    d_value_sum = jnp.einsum(
        "hqk,qhd->khd",
        probabilities.astype(jnp.bfloat16),
        d_attended,
        preferred_element_type=jnp.float32,
    )
    d_query = d_query_parts.reshape(row_count, model_width).astype(jnp.bfloat16)
    d_key = d_key_sum.reshape(row_count, model_width).astype(jnp.bfloat16)
    d_value = d_value_sum.reshape(row_count, model_width).astype(jnp.bfloat16)
    grad_query = inner_rows(act_one, d_query)
    grad_key = inner_rows(act_one, d_key)
    grad_value = inner_rows(act_one, d_value)
    d_act_one = (
        times_transposed(d_query, full_query)
        + times_transposed(d_key, full_key)
        + times_transposed(d_value, full_value)
    )
    norm_one_value, norm_one_back = jax.vjp(layer_norm, rows_float, gain_one_f, bias_one_f)
    d_rows_norm, grad_gain_one, grad_bias_one = norm_one_back(d_act_one)
    grad_tokens = (d_residual + d_rows_norm).astype(jnp.bfloat16)
    summed = lax.psum(
        (
            grad_query,
            grad_key,
            grad_value,
            grad_output,
            grad_router,
            grad_gain_one,
            grad_bias_one,
            grad_gain_two,
            grad_bias_two,
        ),
        ("dp", "expert"),
    )
    share_rows = model_width // lax.axis_size("dp")
    offset = lax.axis_index("dp") * share_rows
    shares = tuple((lax.dynamic_slice_in_dim(member, offset, share_rows, 0) for member in summed))
    return (
        block_out,
        grad_tokens,
        shares[0],
        shares[1],
        shares[2],
        shares[3],
        shares[4],
        shares[5],
        shares[6],
        shares[7],
        shares[8],
        grad_in_part[None],
        grad_out_part[None],
    )


def solution(mesh):
    in_specs = (
        P(("dp", "expert"), None),
        P(("dp", "expert"), None),
        P(("dp", "expert"), None),
        P("dp"),
        P("dp"),
        P("dp"),
        P("dp"),
        P("dp", None),
        P("dp", None),
        P("dp", None),
        P("dp", None),
        P("dp", None),
        P("expert", "dp", None),
        P("expert", "dp", None),
        P("expert", "dp", None),
        P("expert", "dp", None),
        P(("dp", "expert"), None),
    )
    out_specs = (
        P(("dp", "expert"), None),
        P(("dp", "expert"), None),
        P("dp", None),
        P("dp", None),
        P("dp", None),
        P("dp", None),
        P("dp", None),
        P("dp"),
        P("dp"),
        P("dp"),
        P("dp"),
        P("expert", "dp", None),
        P("expert", "dp", None),
    )
    return jax.shard_map(shards, mesh=mesh, in_specs=in_specs, out_specs=out_specs, check_vma=False)
```

profile of v0, /device:TPU:0, one launch (start us, length us, event | category | flops | bytes accessed | tf_op | source)
XLA Modules:
  0.0 1022.1 jit_solution(8854546606733937688)
XLA Ops:
  7.2 2.0 convert_element_type.218
  9.3 1.8 convert_element_type.222
  11.2 1.8 convert_element_type.220
  15.1 3.0 convert_element_type.235
  19.5 3.0 convert_element_type.231
  27.9 14.3 %all-reduce.8 = (bf16[768]{0:T(1024)(128)(2,1)S(1)}, bf16[768]{0:T(1024)(128)(2,1)S(1)}, bf16[768]{0:T(1024)(128)(2,1)S(1)}, bf16[768]{0:T(1024)(128)(2,1)S(1)}) all-reduce(bf16[768]{0:T(1024)(128)(2,1)S(1)} %dynamic-update-slice.1, bf16[768]{0:T(1024)(128)(2,1)S(1)} %dynamic-update-slice, ...), channel_id=1, replica_groups=mesh['dp'=4,'expert'=8] {'dp'}, use_global_device_ids=true, to_apply=%add.3 | all-reduce | flops 3072 | bytes 12288
  42.4 2.4 scatter_custom_fusion
  46.0 1.8 convolution_convert_fusion.3
  48.0 27.4 %all-gather.18.cloned.1.call-done = bf16[768,768]{1,0:T(8,128)(2,1)} async-done(((bf16[192,768]{1,0:T(8,128)(2,1)}), bf16[768,768]{1,0:T(8,128)(2,1)}) %all-gather.18.cloned.1.call-update) | async-done | bytes 1179664 | tf_op jit(solution)/shard_map/all_gather | solution.py:71
  75.4 1.8 convolution_convert_fusion.1
  77.4 29.7 %all-gather.16.cloned.1.call-done = bf16[768,768]{1,0:T(8,128)(2,1)} async-done(((bf16[192,768]{1,0:T(8,128)(2,1)}), bf16[768,768]{1,0:T(8,128)(2,1)}) %all-gather.16.cloned.1.call-update) | async-done | bytes 1179664 | tf_op jit(solution)/shard_map/all_gather | solution.py:70
  107.1 1.8 convolution_convert_fusion.2
  112.2 26.4 %all-gather.20.cloned.1.call-done = bf16[768,768]{1,0:T(8,128)(2,1)} async-done(((bf16[192,768]{1,0:T(8,128)(2,1)}), bf16[768,768]{1,0:T(8,128)(2,1)}) %all-gather.20.cloned.1.call-update) | async-done | bytes 1179664 | tf_op jit(solution)/shard_map/all_gather | solution.py:73
  138.6 1.8 fusion.112
  142.6 3.0 gather_fusion
  145.6 18.6 %all_to_all.20 = bf16[8,2,40,768]{3,2,1,0:T(8,128)(2,1)S(1)} all-to-all(bf16[8,2,40,768]{3,2,1,0:T(8,128)(2,1)S(1)} %bitcast.156), channel_id=1, replica_groups=mesh['dp'=4,'expert'=8] {'expert'}, dimensions={0} | all-to-all | bytes 1966080 | tf_op jit(solution)/shard_map/all_to_all | solution.py:159
  164.1 65.1 %all-gather.26.cloned.1.call-done = bf16[1,768,3072]{2,1,0:T(8,128)(2,1)} async-done(((bf16[1,192,3072]{2,1,0:T(8,128)(2,1)}), bf16[1,768,3072]{2,1,0:T(8,128)(2,1)}) %all-gather.26.cloned.1.call-update) | async-done | bytes 4718608 | tf_op jit(solution)/shard_map/all_gather | solution.py:81
  229.3 89.8 %all-gather.28.cloned.1.call-done = bf16[1,768,3072]{2,1,0:T(8,128)(2,1)} async-done(((bf16[1,192,3072]{2,1,0:T(8,128)(2,1)}), bf16[1,768,3072]{2,1,0:T(8,128)(2,1)}) %all-gather.28.cloned.1.call-update) | async-done | bytes 4718608 | tf_op jit(solution)/shard_map/all_gather | solution.py:83
  319.1 9.6 fusion.11
  328.7 79.8 %all-gather.22.cloned.1.call-done = bf16[1,3072,768]{2,1,0:T(8,128)(2,1)} async-done(((bf16[1,768,768]{2,1,0:T(8,128)(2,1)}), bf16[1,3072,768]{2,1,0:T(8,128)(2,1)}) %all-gather.22.cloned.1.call-update) | async-done | bytes 4718608 | tf_op jit(solution)/shard_map/all_gather | solution.py:82
  408.5 89.4 %all-gather.24.cloned.1.call-done = bf16[1,3072,768]{2,1,0:T(8,128)(2,1)} async-done(((bf16[1,768,768]{2,1,0:T(8,128)(2,1)}), bf16[1,3072,768]{2,1,0:T(8,128)(2,1)}) %all-gather.24.cloned.1.call-update) | async-done | bytes 4718608 | tf_op jit(solution)/shard_map/all_gather | solution.py:84
  497.9 8.1 fusion.42
  507.1 3.7 all-to-all-start.1
  510.8 13.1 %all-gather.4 = bf16[4,192,16]{1,2,0:T(8,128)(2,1)S(1)} all-gather(bf16[1,192,16]{1,2,0:T(8,128)(2,1)S(1)} %convert_bitcast_fusion), channel_id=1, replica_groups=mesh['dp'=4,'expert'=8] {'dp'}, dimensions={0}, use_global_device_ids=true | all-gather | bytes 30720 | tf_op jit(solution)/shard_map/all_gather | solution.py:74
  525.6 3.3 gather_fusion.2
  528.9 1.5 broadcast_in_dim.112
  530.5 3.2 broadcast_in_dim.113
  534.6 2.7 gather_fusion.1
  537.3 2.6 multiply_reduce_fusion.1
  542.3 1.9 multiply_reduce_fusion.7
  546.7 4.6 gather_fusion.3
  552.3 19.1 %all_to_all.21 = bf16[8,2,40,768]{3,2,1,0:T(8,128)(2,1)S(1)} all-to-all(bf16[8,2,40,768]{3,2,1,0:T(8,128)(2,1)S(1)} %multiply_convert_fusion), channel_id=1, replica_groups=mesh['dp'=4,'expert'=8] {'expert'}, dimensions={0} | all-to-all | bytes 1966080 | tf_op jit(solution)/shard_map/all_to_all | solution.py:192
  572.3 12.5 %fusion.7 = bf16[8,2,40,3072]{3,2,0,1:T(8,128)(2,1)} fusion(f32[2,3072,8,40]{1,3,2,0:T(8,128)} %get-tuple-element.49, bf16[1,3072,768]{2,1,0:T(8,128)(2,1)} %all-gather.24.cloned.1.call-done, bf16[1,3072,768]{2,1,0:T(8,128)(2,1)} %all-gather.22.cloned.1.call-done, bf16[8,2,40,768]{3,2,1,0:T(8,128)(2,1)S(1)} %all_to_all.21), kind=kOutput, calls=%fused_computation.19 | convolution fusion | flops 3078094848 | bytes 22216704 | tf_op jit(solution)/shard_map/sekd,efd->sekf/dot_general | solution.py:193
  584.8 6.9 fusion.41
  592.8 3.6 all-to-all-start.3
  597.1 1.9 reshape.502
  600.4 4.3 multiply_reduce_fusion.3
  604.7 6.2 all-to-all-done.3
  610.9 3.0 gather_fusion.4
  614.0 2.2 reshape.503
  616.2 1.9 multiply_reduce_fusion.2
  620.3 2.0 fusion.71
  623.6 1.9 copy.103
  625.5 3.4 fusion.114
  630.3 4.9 fusion.56
  635.2 5.0 fusion.53
  640.2 3.2 fusion.99
  643.4 2.1 fusion.101
  645.5 2.1 fusion.103
  648.7 6.7 bitcast_convert_fusion.1
  656.6 6.5 bitcast_convert_fusion
  664.3 1.8 fusion.115
  666.1 1.8 convolution_add_fusion.2
  668.0 2.0 fusion.108
  670.5 38.8 %all-reduce.6 = (f32[768,16]{0,1:T(8,128)S(1)}, f32[768]{0:T(1024)S(1)}, f32[768]{0:T(1024)S(1)}, f32[768]{0:T(1024)S(1)}, f32[768]{0:T(1024)S(1)}) all-reduce(f32[768,16]{0,1:T(8,128)S(1)} %fusion.116, f32[768]{0:T(1024)S(1)} %get-tuple-element.15, ...), channel_id=1, replica_groups=mesh['dp'=4,'expert'=8] {'dp','expert'}, use_global_device_ids=true, to_apply=%region_27.28 | all-reduce | flops 15360 | bytes 122880 | tf_op jit(solution)/shard_map/psum | solution.py:280
  713.7 122.9 %all-reduce.11.cloned.1.call-done = (f32[768,768]{1,0:T(8,128)}, f32[768,768]{1,0:T(8,128)}, f32[768,768]{1,0:T(8,128)}, f32[768,768]{1,0:T(8,128)}) async-done(((f32[768,768]{1,0:T(8,128)}, f32[768,768]{1,0:T(8,128)}, f32[768,768]{1,0:T(8,128)}, f32[768,768]{1,0:T(8,128)}), (f32[768,768]{1,0:T(8,128)}, f32[768,768]{1,0:T(8,128)}, f32[768,768]{1,0:T(8,128)}, ...) | async-done | bytes 9437200 | tf_op jit(solution)/shard_map/psum | solution.py:280
  836.6 1.9 constant_dynamic-slice_fusion.4
  838.5 1.9 constant_dynamic-slice_fusion.3
  840.5 1.9 constant_dynamic-slice_fusion.2
  842.4 1.9 constant_dynamic-slice_fusion.1
  844.3 79.9 %reduce-scatter.3.cloned.1.call-done = bf16[192,3072]{1,0:T(8,128)(2,1)} async-done(((bf16[768,3072]{1,0:T(8,128)(2,1)}), bf16[192,3072]{1,0:T(8,128)(2,1)}) %reduce-scatter.3.cloned.1.call-update) | async-done | bytes 1179664 | tf_op jit(solution)/shard_map/reduce_scatter | solution.py:209
  924.1 2.9 bitcast_convert_fusion.3
  927.1 85.2 %reduce-scatter.5.cloned.1.call-done = bf16[768,768]{1,0:T(8,128)(2,1)} async-done(((bf16[3072,768]{1,0:T(8,128)(2,1)}), bf16[768,768]{1,0:T(8,128)(2,1)}) %reduce-scatter.5.cloned.1.call-update) | async-done | bytes 1179664 | tf_op jit(solution)/shard_map/reduce_scatter | solution.py:212
  1012.3 2.8 bitcast_convert_fusion.2
  (282 shorter events, 41.9 us)
Async XLA Ops:
  7.2 5.9 copy-start.30
  7.2 6.7 copy-start.17
  7.2 38.8 %all-gather.14.cloned.1.call-start = ((), (), s32[]{:S(2)}) async-start(), calls=%async_computation.6 | async-start | bytes 1474560 | tf_op jit(solution)/shard_map/all_gather | solution.py:72
  9.2 66.2 %all-gather.18.cloned.1.call-start = ((), (), s32[]{:S(2)}) async-start(), calls=%async_computation.8 | async-start | bytes 1474560 | tf_op jit(solution)/shard_map/all_gather | solution.py:71
  11.1 96.0 %all-gather.16.cloned.1.call-start = ((), (), s32[]{:S(2)}) async-start(), calls=%async_computation.7 | async-start | bytes 1474560 | tf_op jit(solution)/shard_map/all_gather | solution.py:70
  13.0 125.6 %all-gather.20.cloned.1.call-start = ((), (), s32[]{:S(2)}) async-start(), calls=%async_computation.9 | async-start | bytes 1474560 | tf_op jit(solution)/shard_map/all_gather | solution.py:73
  13.8 215.4 %all-gather.26.cloned.1.call-start = ((), (), s32[]{:S(2)}) async-start(), calls=%async_computation.14 | async-start | bytes 5898240 | tf_op jit(solution)/shard_map/all_gather | solution.py:81
  15.1 304.0 %all-gather.28.cloned.1.call-start = ((), (), s32[]{:S(2)}) async-start(), calls=%async_computation.15 | async-start | bytes 5898240 | tf_op jit(solution)/shard_map/all_gather | solution.py:83
  18.1 390.3 %all-gather.22.cloned.1.call-start = ((), (), s32[]{:S(2)}) async-start(), calls=%async_computation.12 | async-start | bytes 5898240 | tf_op jit(solution)/shard_map/all_gather | solution.py:82
  19.3 6.4 copy-start.74
  19.3 6.4 copy-start.75
  19.3 6.5 copy-start.76
  19.3 6.5 copy-start.77
  19.3 6.5 copy-start.78
  19.4 26.1 %copy-start = (bf16[256,768]{1,0:T(8,128)(2,1)S(1)}, bf16[256,768]{1,0:T(8,128)(2,1)}, u32[]{:S(2)}) copy-start(bf16[256,768]{1,0:T(8,128)(2,1)} %param.17) | copy-start | bytes 1179652
  19.4 26.5 %copy-start.73 = (s32[1,256]{1,0:T(1,128)S(1)}, s32[1,256]{1,0:T(1,128)}, u32[]{:S(2)}) copy-start(s32[1,256]{1,0:T(1,128)} %param.18) | copy-start | bytes 3076
  19.4 478.5 %all-gather.24.cloned.1.call-start = ((), (), s32[]{:S(2)}) async-start(), calls=%async_computation.13 | async-start | bytes 5898240 | tf_op jit(solution)/shard_map/all_gather | solution.py:84
  42.3 64.8 %copy-start.40 = (f32[768]{0:T(1024)}, f32[768]{0:T(1024)S(1)}, u32[]{:S(2)}) copy-start(f32[768]{0:T(1024)S(1)} %convert_element_type.216) | copy-start | bytes 9220
  42.3 98.4 %copy-start.42 = (f32[768]{0:T(1024)}, f32[768]{0:T(1024)S(1)}, u32[]{:S(2)}) copy-start(f32[768]{0:T(1024)S(1)} %convert_element_type.238) | copy-start | bytes 9220
  45.4 97.2 %copy-start.49 = (s32[1024]{0:T(1024)}, s32[1024]{0:T(1024)S(1)}, u32[]{:S(2)}) copy-start(s32[1024]{0:T(1024)S(1)} %get-tuple-element.53) | copy-start | bytes 12292
  45.6 61.5 %copy-start.38 = (f32[256]{0:T(256)}, f32[256]{0:T(256)S(1)}, u32[]{:S(2)}) copy-start(f32[256]{0:T(256)S(1)} %broadcast_multiply_fusion.1) | copy-start | bytes 3076
  45.8 31.6 %copy-start.66 = (f32[256]{0:T(256)}, f32[256]{0:T(256)S(1)}, u32[]{:S(2)}) copy-start(f32[256]{0:T(256)S(1)} %fusion.68) | copy-start | bytes 3076
  45.9 61.2 %copy-start.47 = (f32[256]{0:T(256)}, f32[256]{0:T(256)S(1)}, u32[]{:S(2)}) copy-start(f32[256]{0:T(256)S(1)} %fusion.88) | copy-start | bytes 3076
  46.0 63.1 %copy-start.33 = (pred[256,256]{0,1:T(8,128)(4,1)}, pred[256,256]{0,1:T(8,128)(4,1)S(1)}, u32[]{:S(2)}) copy-start(pred[256,256]{0,1:T(8,128)(4,1)S(1)} %fusion.70) | copy-start | bytes 196612
  48.0 62.3 %copy-start.23 = (bf16[256,768]{0,1:T(8,128)(2,1)}, bf16[256,768]{0,1:T(8,128)(2,1)S(1)}, u32[]{:S(2)}) copy-start(bf16[256,768]{0,1:T(8,128)(2,1)S(1)} %copy.85) | copy-start | bytes 1179652
  77.4 32.4 %copy-start.24 = (bf16[256,768]{0,1:T(8,128)(2,1)}, bf16[256,768]{0,1:T(8,128)(2,1)S(1)}, u32[]{:S(2)}) copy-start(bf16[256,768]{0,1:T(8,128)(2,1)S(1)} %copy.87) | copy-start | bytes 1179652
  112.2 28.5 %copy-start.19 = (bf16[12,64,256]{2,1,0:T(8,128)(2,1)}, bf16[12,64,256]{2,1,0:T(8,128)(2,1)S(1)}, u32[]{:S(2)}) copy-start(bf16[12,64,256]{2,1,0:T(8,128)(2,1)S(1)} %fusion.49) | copy-start | bytes 1179652
  164.1 164.6 %copy-start.26 = (bf16[8,2,40,768]{3,2,1,0:T(8,128)(2,1)}, bf16[8,2,40,768]{3,2,1,0:T(8,128)(2,1)S(1)}, u32[]{:S(2)}) copy-start(bf16[8,2,40,768]{3,2,1,0:T(8,128)(2,1)S(1)} %all_to_all.20) | copy-start | bytes 2949124
  506.0 4.7 copy-start.64
  506.0 18.0 %copy-start.52 = (s32[512]{0:T(512)S(1)}, s32[512]{0:T(512)}, u32[]{:S(2)}) copy-start(s32[512]{0:T(512)} %copy-done.51) | copy-start | bytes 6148
  506.0 19.5 %copy-start.5 = (bf16[256,768]{1,0:T(8,128)(2,1)S(1)}, bf16[256,768]{1,0:T(8,128)(2,1)}, u32[]{:S(2)}) copy-start(bf16[256,768]{1,0:T(8,128)(2,1)} %param.33) | copy-start | bytes 1179652
  506.0 19.5 %copy-start.50 = (s32[1024]{0:T(1024)S(1)}, s32[1024]{0:T(1024)}, u32[]{:S(2)}) copy-start(s32[1024]{0:T(1024)} %copy-done.49) | copy-start | bytes 12292
  507.1 27.5 %all-to-all-start.1 = ((bf16[8,2,40,768]{3,2,1,0:T(8,128)(2,1)}), bf16[8,2,40,768]{3,2,1,0:T(8,128)(2,1)S(1)}, u32[]{:S(2)}, u32[]{:S(2)}) async-start(bf16[8,2,40,768]{3,2,1,0:T(8,128)(2,1)} %copy.94), calls=%async_computation.1 | async-start | bytes 1966080 | tf_op jit(solution)/shard_map/all_to_all | solution.py:167
  524.0 9.6 copy-start.34
  528.9 4.7 copy-start.72
  528.9 4.7 copy-start.11
  528.9 4.9 copy-start.57
  537.3 14.8 %copy-start.8 = (f32[640,768]{1,0:T(8,128)S(1)}, f32[640,768]{1,0:T(8,128)}, u32[]{:S(2)}) copy-start(f32[640,768]{1,0:T(8,128)} %gather_fusion.2) | copy-start | bytes 5898244
  552.1 32.7 %slice-start = ((s8[4718592]{0:T(1024)(128)(4,1)}), s8[4194304]{0:T(1024)(128)(4,1)S(1)}, s32[]{:S(2)}) async-start(s8[4718592]{0:T(1024)(128)(4,1)} %bitcast.178), calls=%async_computation.17 | async-start | bytes 8388608
  572.3 12.5 %slice-start.1 = ((s8[4718592]{0:T(1024)(128)(4,1)}), s8[524288]{0:T(1024)(128)(4,1)S(1)}, s32[]{:S(2)}) async-start(s8[4718592]{0:T(1024)(128)(4,1)} %bitcast.178), calls=%async_computation.18 | async-start | bytes 1048576
  591.7 4.7 copy-start.32
  591.7 4.7 copy-start.37
  591.7 4.7 copy-start.45
  591.7 5.3 copy-start.9
  591.7 7.2 copy-start.55
  591.7 7.2 copy-start.70
  592.8 18.2 %all-to-all-start.3 = ((bf16[8,2,40,768]{3,2,1,0:T(8,128)(2,1)}), bf16[8,2,40,768]{3,2,1,0:T(8,128)(2,1)S(1)}, u32[]{:S(2)}, u32[]{:S(2)}) async-start(bf16[8,2,40,768]{3,2,1,0:T(8,128)(2,1)} %copy.100), calls=%async_computation.3 | async-start | bytes 1966080 | tf_op jit(solution)/shard_map/all_to_all | solution.py:216
  596.3 240.3 %all-reduce.11.cloned.1.call-start = ((), (), s32[]{:S(2)}) async-start(), calls=%async_computation.16 | async-start | bytes 18874368 | tf_op jit(solution)/shard_map/psum | solution.py:280
  614.0 4.1 copy-start.35
  614.0 4.2 copy-start.43
  614.0 4.2 copy-start.54
  614.0 4.2 copy-start.61
  614.0 5.2 copy-start.69
  622.3 6.6 copy-start.2
  625.5 3.4 copy-start.46
  635.2 5.0 copy-start.39
  640.2 5.3 copy-start.22
  647.5 276.6 %reduce-scatter.3.cloned.1.call-start = ((), (), s32[]{:S(2)}) async-start(), calls=%async_computation.10 | async-start | bytes 5898240 | tf_op jit(solution)/shard_map/reduce_scatter | solution.py:209
  655.4 356.9 %reduce-scatter.5.cloned.1.call-start = ((), (), s32[]{:S(2)}) async-start(), calls=%async_computation.11 | async-start | bytes 5898240 | tf_op jit(solution)/shard_map/reduce_scatter | solution.py:212
  663.2 4.8 copy-start.14
  666.1 3.9 copy-start.67
  668.0 44.6 %copy-start.4 = (f32[256,768]{1,0:T(8,128)S(1)}, f32[256,768]{1,0:T(8,128)}, u32[]{:S(2)}) copy-start(f32[256,768]{1,0:T(8,128)} %copy-done.3) | copy-start | bytes 2359300
  668.0 44.6 %copy-start.7 = (bf16[256,768]{1,0:T(8,128)(2,1)S(1)}, bf16[256,768]{1,0:T(8,128)(2,1)}, u32[]{:S(2)}) copy-start(bf16[256,768]{1,0:T(8,128)(2,1)} %param.33) | copy-start | bytes 1179652
  668.0 44.6 %copy-start.59 = (f32[256]{0:T(256)S(1)}, f32[256]{0:T(256)}, u32[]{:S(2)}) copy-start(f32[256]{0:T(256)} %copy-done.58) | copy-start | bytes 3076
  (30 other events, 61.7 us)
Sparse Core Ops, SparseCore 0:
  10.1 33.5 all-gather.13
  45.8 29.5 all-gather.17
  77.6 29.4 all-gather.15
  109.1 29.4 all-gather.19
  140.6 88.6 all-gather.25
  231.3 87.7 all-gather.27
  320.7 87.7 all-gather.21
  410.1 87.7 all-gather.23
  647.7 188.9 all-reduce.10
  838.8 85.3 reduce-scatter.2
  926.4 85.7 reduce-scatter.4
where the time goes:
time: 1030 us; the launch traced here: 1020 us
  waiting for transfers between devices  702 us (68%)
  blocking collectives  104 us (10%)
  matrix products  91.2 us (9%)
  local copies, waits for them, and re-layouts  60.8 us (6%)
  other arithmetic  40.4 us (4%)
  between operations  16.2 us (2%)
    psum x1, waiting for transfers between devices, shards(): lax.psum((grad_query, grad_key, grad_value, grad_output, grad_router, gra...  123 us
    all_gather x1, waiting for transfers between devices, shards(): lax.all_gather(new_in[0].astype(jnp.bfloat16), 'dp', axis=0, tiled=True)  89.8 us
    all_gather x1, waiting for transfers between devices, shards(): lax.all_gather(new_out[0].astype(jnp.bfloat16), 'dp', axis=0, tiled=True)  89.4 us
    reduce_scatter x1, waiting for transfers between devices, shards(): lax.psum_scatter(grad_out_full.astype(jnp.bfloat16), 'dp', scatter_dimens...  85.2 us
    reduce_scatter x1, waiting for transfers between devices, shards(): lax.psum_scatter(grad_in_full.astype(jnp.bfloat16), 'dp', scatter_dimensi...  79.9 us
    all_gather x1, waiting for transfers between devices, shards(): lax.all_gather(frozen_out[0].astype(jnp.bfloat16), 'dp', axis=0, tiled=True)  79.8 us
    all_gather x1, waiting for transfers between devices, shards(): lax.all_gather(frozen_in[0].astype(jnp.bfloat16), 'dp', axis=0, tiled=True)  65.1 us
    psum x1, blocking collectives, shards(): lax.psum((grad_query, grad_key, grad_value, grad_output, grad_router, gra...  38.8 us
  transfers between devices with their start and end apart: 13, of which 11 were waited for; matrix products, arithmetic and copies ran while one was open for 9% of the time, Pallas kernels for 0%

commit v1 on v0

v1 whole, which is shorter than its diff:
```python
import functools

import jax
import jax.numpy as jnp
from jax import lax
from jax.experimental import pallas as pl
from jax.experimental.pallas import tpu as pltpu
from jax.sharding import PartitionSpec as P

HEADS = 12
HEAD = 64
NORM_EPS = 1e-05
MASKED = -1e30
MESH = pl.DeviceIdType.MESH
BF = jnp.bfloat16
F32 = jnp.float32
VMEM_LIMIT = 60 * 1024 * 1024


class Place:
    def __init__(self, planes, experts):
        self.planes, self.experts = planes, experts
        self.z = lax.axis_index("dp")
        self.i = lax.axis_index("expert")
        self.core = lax.rem(self.i, 2)
        self.chip = lax.div(self.i, 2)
        self.xb = lax.rem(self.chip, 2)
        self.yb = lax.rem(lax.div(self.i, 4), 2)
        self.sib = self.i + 1 - 2 * self.core
        self.xn = self.i + 2 - 4 * self.xb
        self.yn = self.i + 4 - 8 * self.yb
        self.chips = planes * (experts // 2)
        self.me = self.z * (experts // 2) + self.chip


def send_to(src, dst, send_sem, recv_sem, z, i):
    return pltpu.make_async_remote_copy(
        src_ref=src,
        dst_ref=dst,
        send_sem=send_sem,
        recv_sem=recv_sem,
        device_id={"dp": z, "expert": i},
        device_id_type=MESH,
    )


def greet(at):
    barrier = pltpu.get_barrier_semaphore()
    count = at.planes * at.experts
    own = at.z * at.experts + at.i

    def signal(step, carry):
        target = lax.rem(own + step, count)
        pl.semaphore_signal(
            barrier,
            inc=1,
            device_id={"dp": lax.div(target, at.experts), "expert": lax.rem(target, at.experts)},
            device_id_type=MESH,
        )
        return carry

    lax.fori_loop(1, count, signal, 0)
    return lambda: pl.semaphore_wait(barrier, count - 1)


def any_spec():
    return pl.BlockSpec(memory_space=pl.ANY)


def vmem_spec():
    return pl.BlockSpec(memory_space=pltpu.VMEM)


NN = ((1,), (0,))
NT = ((1,), (1,))
TN = ((0,), (0,))


def dot(left, right, contract, out=F32):
    return lax.dot_general(
        left, right, ((contract[0], contract[1]), ((), ())), preferred_element_type=F32
    ).astype(out)


def exact_dot(left, right, contract):
    return lax.dot_general(
        left, right, ((contract[0], contract[1]), ((), ())),
        preferred_element_type=F32, precision=lax.Precision.HIGHEST,
    )


def norm_parts(rows):
    centred = rows - jnp.mean(rows, axis=-1, keepdims=True)
    variance = jnp.mean(centred * centred, axis=-1, keepdims=True)
    scale = lax.rsqrt(variance + NORM_EPS)
    return centred * scale, scale


def norm_back(rows, gain, grad):
    unit, scale = norm_parts(rows)
    scaled = grad * gain
    inner = scaled - jnp.mean(scaled, axis=-1, keepdims=True)
    inner = inner - unit * jnp.mean(scaled * unit, axis=-1, keepdims=True)
    return scale * inner, jnp.sum(grad * unit, axis=0, keepdims=True), jnp.sum(grad, axis=0, keepdims=True)


def slot_places(slot, slots):
    lanes = lax.broadcasted_iota(jnp.int32, (slot[0].shape[0], slots), 1).astype(F32)
    return [(lanes == one).astype(F32).astype(BF) for one in slot]


def slot_values(aux, table, padded, chips):
    rows = aux.shape[0]
    low = lax.broadcasted_iota(jnp.int32, (rows, chips), 1).astype(F32) * padded
    lanes = lax.broadcasted_iota(jnp.int32, (rows, table.shape[1]), 1).astype(F32)
    found = []
    for k in range(2):
        slot = aux[:, 2 + k:3 + k]
        mine = jnp.logical_and(slot >= low, slot < low + padded).astype(F32)
        position = slot - jnp.sum(mine * low, axis=1, keepdims=True)
        picked = exact_dot(mine, table, NN)
        found.append(jnp.sum(jnp.where(lanes == position, picked, 0.0), axis=1, keepdims=True))
    return found


def front_kernel(planes, experts, capacity, padded, nrouter,
                 tokens, cot, segs, routes, router, g1, b1, g2, b2, wq, wk, wv, wo, fi, fo, ni, no,
                 wd, pk, win, wout, act_one, act_two, q, k, v, att, resid, probs, aux, ga,
                 xland, dland, gland,
                 packs, allow, xsend, esend, gsend, dstage, istage, ostage, ibf, obf,
                 ld, zs, zr, ps, pr, gs, gr, es, er, fs, fr, ts, tr, tl, sa, ra):
    at = Place(planes, experts)
    z, i, core = at.z, at.i, at.core
    rows, width = tokens.shape
    chips = at.chips
    per_plane = experts // 2
    share = dstage.shape[1]
    quarter = share // 4
    half = width // 2
    fhalf = istage.shape[2] // 2
    oshare = ostage.shape[1]
    ohalf = oshare // 2
    pairs = width // 128
    spot = lax.rem(i, 8)
    base = i - spot
    loads = [pltpu.make_async_copy(w, dstage.at[m], ld.at[m]) for m, w in enumerate((wq, wk, wv, wo))]
    loads += [
        pltpu.make_async_copy(fi.at[0], istage.at[0], ld.at[4]),
        pltpu.make_async_copy(ni.at[0], istage.at[1], ld.at[5]),
        pltpu.make_async_copy(fo.at[0], ostage.at[0], ld.at[6]),
        pltpu.make_async_copy(no.at[0], ostage.at[1], ld.at[7]),
    ]
    for load in loads:
        load.start()
    met = greet(at)
    zrow = pl.multiple_of(z * share, share)
    for m in range(4):
        loads[m].wait()
        wd[m, pl.ds(zrow, share), :] = dstage[m].astype(BF)
    packs[z, 0:nrouter, :] = router[...].astype(BF)
    norm_row = lax.broadcasted_iota(jnp.int32, (16, share), 0)
    norms = jnp.zeros((16, share), F32)
    for n, values in enumerate((g1, b1, g2, b2)):
        norms = jnp.where(norm_row == n, values[...], norms)
    packs[z, nrouter:nrouter + 16, :] = norms.astype(BF)
    met()

    def block(plane, row_quarter, column_half):
        return wd.at[
            :,
            pl.ds(pl.multiple_of(plane * share + row_quarter * quarter, 16), quarter),
            pl.ds(pl.multiple_of(column_half * half, 128), half),
        ]

    rq = 2 * at.yb + core
    rqy = 2 * (1 - at.yb) + core
    rqs = 2 * at.yb + 1 - core
    rqys = 2 * (1 - at.yb) + 1 - core
    xb, xo = at.xb, 1 - at.xb
    started = []
    for j in range(1, planes):
        zt = lax.rem(z + j, planes)
        mine = block(z, rq, xb)
        copy = send_to(mine, mine, zs.at[j - 1], zr.at[j - 1], zt, i)
        copy.start()
        started.append(copy)
        copy = send_to(packs.at[z], packs.at[z], ps.at[j - 1], pr.at[j - 1], zt, i)
        copy.start()
        started.append(copy)

    def cast(source, target, kind, chunk):
        def step(n, carry):
            part = pl.ds(pl.multiple_of(n * chunk, chunk), chunk)
            target[kind, part, :] = source[kind, part, :].astype(BF)
            return carry

        lax.fori_loop(0, source.shape[1] // chunk, step, 0)

    def in_block(plane, h):
        return win.at[
            pl.ds(pl.multiple_of(plane * share, 16), share),
            pl.ds(pl.multiple_of(h * fhalf, 128), fhalf),
        ]

    def out_block(plane, h):
        return wout.at[pl.ds(pl.multiple_of(plane * oshare + h * ohalf, 16), ohalf), :]

    remote_sends = []

    def ship(kind, h, which):
        zh = 3 * core if kind == 0 else 1 + core
        remote = jnp.logical_or(zh != z, core != h)
        src = (
            ibf.at[kind, :, pl.ds(h * fhalf, fhalf)]
            if which == 0
            else obf.at[kind, pl.ds(h * ohalf, ohalf), :]
        )
        dst = in_block(z, h) if which == 0 else out_block(z, h)
        far = send_to(src, dst, es.at[kind, h, which], er.at[z, which], zh, 2 * at.chip + h)
        near = pltpu.make_async_copy(src, dst, er.at[z, which])
        pl.when(remote)(far.start)
        pl.when(jnp.logical_not(remote))(near.start)
        remote_sends.append((remote, far))

    for n, kind in ((4, 0), (5, 1)):
        loads[n].wait()
        cast(istage, ibf, kind, 16)
        for h in range(2):
            ship(kind, h, 0)

    shift = experts.bit_length() - 1
    above = lax.broadcasted_iota(jnp.int32, (rows, rows), 0)
    across = lax.broadcasted_iota(jnp.int32, (rows, rows), 1)
    segment = segs[...].astype(F32)
    fact_row = lax.broadcasted_iota(jnp.int32, (8, rows), 0)
    facts = jnp.zeros((8, rows), F32)
    for n, values in enumerate((routes[0:1, :].astype(F32), routes[1:2, :].astype(F32), segment)):
        facts = jnp.where(fact_row == n, values, facts)
    fact_columns = dot((above == across).astype(F32).astype(BF), facts.astype(BF), NT)
    route_columns = [fact_columns[:, n:n + 1] for n in range(2)]
    route = fact_columns.astype(jnp.int32)
    expert = jnp.bitwise_and(route, experts - 1)
    kind = jnp.right_shift(route, shift)
    host_plane = jnp.where(jnp.bitwise_and(expert, 1) == 0, kind, 3 - kind)
    host = host_plane * per_plane + jnp.right_shift(expert, 1)
    chip_iota = lax.broadcasted_iota(jnp.int32, (rows, chips), 1)
    chosen = [(chip_iota == host[:, n:n + 1]).astype(F32) for n in range(2)]
    earlier = (across < above).astype(F32).astype(BF)
    before = dot(earlier, (chosen[0] + chosen[1]).astype(BF), NN)
    position = [jnp.sum(one * before, axis=1, keepdims=True) for one in chosen]
    slot = [
        jnp.where(position[n] < capacity, host[:, n:n + 1].astype(F32) * padded + position[n], -1.0)
        for n in range(2)
    ]
    place = slot_places(slot, chips * padded)
    both = place[0] + place[1]

    def fill(target, values):
        sent = dot(both, values, TN)
        for n in range(chips):
            target[n] = sent[n * padded:(n + 1) * padded].astype(BF)

    def token_copy(src, dst, which, step):
        target = lax.rem(at.me + step, chips)
        zt, it = lax.div(target, per_plane), 2 * lax.rem(target, per_plane) + core
        return send_to(src.at[target], dst.at[at.me], ts.at[which, step], tr.at[which, step], zt, it)

    def token_start(src, dst, which):
        pltpu.make_async_copy(src.at[at.me], dst.at[at.me], tl.at[which]).start()

        def step(n, carry):
            token_copy(src, dst, which, n).start()
            return carry

        lax.fori_loop(1, chips, step, 0)

    def token_finish(src, dst, which):
        def step(n, carry):
            source = lax.rem(at.me + chips - n, chips)
            send_to(
                src.at[source], dst.at[source], ts.at[which, n], tr.at[which, n], z, i
            ).wait_recv()
            token_copy(src, dst, which, n).wait_send()
            return carry

        lax.fori_loop(1, chips, step, 0)
        pltpu.make_async_copy(src.at[at.me], dst.at[at.me], tl.at[which]).wait()

    fill(esend, cot[...])
    token_start(esend, dland, 0)
    for n, kind in ((6, 0), (7, 1)):
        loads[n].wait()
        cast(ostage, obf, kind, 32)
        for h in range(2):
            ship(kind, h, 1)
    same = jnp.logical_and(fact_columns[:, 2:3] == segment, across <= above)
    allow[...] = same.astype(F32)

    def pass_on(src, j, step, target):
        copy = send_to(src, src, gs.at[j - 1, step], gr.at[j - 1, step], z, target)
        copy.start()
        started.append(copy)

    def landed(dst, j, step):
        send_to(dst, dst, gs.at[j - 1, step], gr.at[j - 1, step], z, i).wait_recv()

    for j in range(1, planes):
        zz = lax.rem(z + planes - j, planes)
        mine = block(zz, rq, xb)
        send_to(mine, mine, zs.at[j - 1], zr.at[j - 1], z, i).wait_recv()
        pass_on(mine, j, 0, at.xn)
        pass_on(mine, j, 1, at.yn)
        pass_on(mine, j, 2, at.sib)
        send_to(packs.at[zz], packs.at[zz], ps.at[j - 1], pr.at[j - 1], z, i).wait_recv()
    pk[...] = jnp.concatenate([packs[p] for p in range(planes)], axis=1)

    x = tokens[...].astype(F32)
    gain = pk[nrouter:nrouter + 1, :].astype(F32)
    bias = pk[nrouter + 1:nrouter + 2, :].astype(F32)
    act_one[...] = (norm_parts(x)[0] * gain + bias).astype(BF)

    for j in range(1, planes):
        zz = lax.rem(z + planes - j, planes)
        bx, by = block(zz, rq, xo), block(zz, rqy, xb)
        landed(bx, j, 0)
        landed(by, j, 1)
        onward = block(zz, rq + core * (rqy - rq), xo + core * (xb - xo))
        pass_on(onward, j, 3, at.yn + core * (at.xn - at.yn))
        pass_on(bx, j, 4, at.sib)
        pass_on(by, j, 5, at.sib)
    for j in range(1, planes):
        zz = lax.rem(z + planes - j, planes)
        bd = block(zz, rqy, xo)
        landed(bd, j, 3)
        pass_on(bd, j, 6, at.sib)
    for j in range(1, planes):
        zz = lax.rem(z + planes - j, planes)
        landed(block(zz, rqs, xb), j, 2)
        landed(block(zz, rqs, xo), j, 4)
        landed(block(zz, rqys, xb), j, 5)
        landed(block(zz, rqys, xo), j, 6)

    def act_copy(step, whole):
        target = lax.rem(spot + step, 8)
        src = act_one if whole else att
        return target, send_to(src, ga.at[spot], sa.at[step], ra.at[step], z, base + target)

    def act_near(whole):
        return pltpu.make_async_copy(act_one if whole else att, ga.at[spot], tl.at[3])

    for step in range(1, 8):
        target, copy = act_copy(step, True)
        pl.when(target < pairs)(copy.start)
    pl.when(spot < pairs)(act_near(True).start)

    one = act_one[...]
    q[...] = dot(one, wd[0], NN, BF)
    k[...] = dot(one, wd[1], NN, BF)
    v[...] = dot(one, wd[2], NN, BF)
    lane = lax.broadcasted_iota(jnp.int32, (rows, 128), 1)
    masks = [(lane < HEAD).astype(F32).astype(BF), (lane >= HEAD).astype(F32).astype(BF)]
    score_scale = HEAD ** (-0.5)

    def head_pair(n, carry):
        cols = pl.ds(pl.multiple_of(n * 128, 128), 128)
        q2, k2, v2 = q[:, cols], k[:, cols], v[:, cols]
        total = jnp.zeros((rows, 128), F32)
        for side in range(2):
            scores = dot(q2 * masks[side], k2, NT) * score_scale
            scores = jnp.where(allow[...] > 0.5, scores, MASKED)
            expo = jnp.exp(scores - jnp.max(scores, axis=-1, keepdims=True))
            p = expo / jnp.sum(expo, axis=-1, keepdims=True)
            probs[2 * n + side] = p
            total += dot(p.astype(BF), v2 * masks[side], NN)
        att[:, cols] = total.astype(BF)
        return carry

    lax.fori_loop(0, pairs, head_pair, 0)
    residual = x + dot(att[...], wd[3], NN)
    resid[...] = residual
    gain = pk[nrouter + 2:nrouter + 3, :].astype(F32)
    bias = pk[nrouter + 3:nrouter + 4, :].astype(F32)
    two = (norm_parts(residual)[0] * gain + bias).astype(BF)
    act_two[...] = two
    fill(xsend, two)
    token_start(xsend, xland, 1)
    for step in range(1, 8):
        target, copy = act_copy(step, False)
        pl.when(target >= pairs)(copy.start)
    pl.when(spot >= pairs)(act_near(False).start)

    logits = dot(two, pk[0:nrouter, :], NT)
    route_iota = lax.broadcasted_iota(jnp.int32, (rows, nrouter), 1)
    picked = [
        jnp.sum(jnp.where(route_iota == route[:, n:n + 1], logits, 0.0), axis=1, keepdims=True)
        for n in range(2)
    ]
    top = jnp.maximum(picked[0], picked[1])
    lifted = [jnp.exp(one_pick - top) for one_pick in picked]
    gates = [one_lift / (lifted[0] + lifted[1]) for one_lift in lifted]
    values = jnp.zeros((rows, 128), F32)
    for n, column in enumerate(gates + slot + route_columns):
        values = jnp.where(lane == n, column, values)
    aux[...] = values
    lanes = lane.astype(F32)
    table = jnp.zeros((chips, 128), F32)
    for n in range(2):
        kept = jnp.logical_and(lanes == position[n], position[n] < capacity)
        table += exact_dot(chosen[n], jnp.where(kept, gates[n], 0.0), TN)
    for n in range(chips):
        gsend[n] = table[n:n + 1]
    token_start(gsend, gland, 2)

    def hand_on(plane, which):
        blk = in_block(plane, core) if which == 0 else out_block(plane, core)
        send_to(blk, blk, es.at[0, 0, which], er.at[plane, which], z, i).wait_recv()
        copy = send_to(blk, blk, fs.at[plane, which], fr.at[plane, which], z, at.sib)
        copy.start()
        started.append(copy)

    for which in range(2):
        for plane in range(planes):
            hand_on(plane, which)
    for src, dst, which in ((esend, dland, 0), (xsend, xland, 1), (gsend, gland, 2)):
        token_finish(src, dst, which)
    for step in range(1, 8):
        source = lax.rem(spot + 8 - step, 8)
        send_to(act_one, ga.at[source], sa.at[step], ra.at[step], z, i).wait_recv()
        act_copy(step, True)[1].wait_send()
    act_near(True).wait()
    for which in range(2):
        for plane in range(planes):
            blk = in_block(plane, 1 - core) if which == 0 else out_block(plane, 1 - core)
            send_to(blk, blk, fs.at[plane, which], fr.at[plane, which], z, i).wait_recv()
    for copy in started:
        copy.wait_send()
    for remote, far in remote_sends:
        pl.when(remote)(far.wait_send)


def front(planes, experts, capacity, padded, nrouter, tokens, cot, segment_ids, routes, router, norms,
          wq, wk, wv, wo, fi, fo, ni, no):
    rows, width = tokens.shape
    share = wq.shape[0]
    ff = fi.shape[2]
    oshare = fo.shape[1]
    chips = planes * experts // 2
    dma = pltpu.SemaphoreType.DMA
    vm = pltpu.VMEM
    sds = jax.ShapeDtypeStruct
    flat = sds((rows, width), BF)
    slab = sds((chips, padded, width), BF)
    return pl.pallas_call(
        functools.partial(front_kernel, planes, experts, capacity, padded, nrouter),
        out_shape=(
            sds((4, width, width), BF),
            sds((nrouter + 16, width), BF),
            sds((width, ff), BF),
            sds((ff, width), BF),
            flat, flat, flat, flat, flat, flat,
            sds((rows, width), F32),
            sds((HEADS, rows, rows), F32),
            sds((rows, 128), F32),
            sds((8, rows, width), BF),
            slab,
            slab,
            sds((chips, 1, 128), F32),
        ),
        in_specs=[vmem_spec()] * 9 + [any_spec()] * 8,
        out_specs=(vmem_spec(), vmem_spec(), any_spec(), any_spec()) + (vmem_spec(),) * 9 + (any_spec(),) * 4,
        scratch_shapes=[
            vm((planes, nrouter + 16, share), BF),
            vm((rows, rows), F32),
            vm((chips, padded, width), BF),
            vm((chips, padded, width), BF),
            vm((chips, 1, 128), F32),
            vm((4, share, width), F32),
            vm((2, share, ff), F32),
            vm((2, oshare, width), F32),
            vm((2, share, ff), BF),
            vm((2, oshare, width), BF),
            dma((8,)),
            dma((planes - 1,)), dma((planes - 1,)), dma((planes - 1,)), dma((planes - 1,)),
            dma((planes - 1, 7)), dma((planes - 1, 7)),
            dma((2, 2, 2)), dma((planes, 2)), dma((planes, 2)), dma((planes, 2)),
            dma((3, chips)), dma((3, chips)), dma((4,)), dma((8,)), dma((8,)),
        ],
        compiler_params=pltpu.CompilerParams(
            collective_id=0, has_side_effects=True, vmem_limit_bytes=VMEM_LIMIT
        ),
        name="front",
    )(tokens, cot, segment_ids, routes.T, router.T, *[norm.reshape(1, share) for norm in norms],
      wq, wk, wv, wo, fi, fo, ni, no)


GELU_SCALE = 0.7978845608028654
GELU_CUBE = 0.044715


def mid_kernel(planes, experts, padded, blocks,
               x, do, gate, win, wout,
               ysend, gi, go, dxland, dgland,
               wi, wo, dy, hid, dpre, dxsend, dgsend,
               ls, ts, tr, tl):
    at = Place(planes, experts)
    z, i, core = at.z, at.i, at.core
    per_plane = experts // 2
    chunk = per_plane * padded
    width = x.shape[1]
    ff = wi.shape[1]
    wide = ff // blocks
    load_i = pltpu.make_async_copy(win, wi, ls.at[0])
    load_o = pltpu.make_async_copy(wout, wo, ls.at[1])
    load_i.start()
    load_o.start()
    met = greet(at)
    lane = lax.broadcasted_iota(jnp.int32, (padded, 128), 1)
    diagonal = lane == lax.broadcasted_iota(jnp.int32, (padded, 128), 0)
    load_i.wait()
    load_o.wait()
    met()

    def copies(plane, n):
        target = plane * per_plane + n
        there = 2 * n + core
        rows = dxland.at[pl.ds(pl.multiple_of(at.me * padded, 8), padded), :]
        return [
            send_to(dxsend.at[target], rows, ts.at[0, target], tr.at[0, at.me], plane, there),
            send_to(dgsend.at[target], dgland.at[at.me], ts.at[1, target], tr.at[1, at.me], plane, there),
        ]

    def own_copies():
        rows = dxland.at[pl.ds(pl.multiple_of(at.me * padded, 8), padded), :]
        return [
            pltpu.make_async_copy(dxsend.at[at.me], rows, tl.at[0]),
            pltpu.make_async_copy(dgsend.at[at.me], dgland.at[at.me], tl.at[1]),
        ]

    def work(plane):
        rows = pl.ds(pl.multiple_of(plane * chunk, 16), chunk)
        x_c = x[rows, :]
        do_c = do[rows, :].astype(F32)
        column = jnp.concatenate(
            [
                jnp.sum(jnp.where(diagonal, gate[plane * per_plane + n], 0.0), axis=1, keepdims=True)
                for n in range(per_plane)
            ],
            axis=0,
        )
        dy_c = (do_c * column).astype(BF)
        dy[rows, :] = dy_c
        y_sum = jnp.zeros((chunk, width), F32)
        dx_sum = jnp.zeros((chunk, width), F32)
        for b in range(blocks):
            cols = slice(b * wide, (b + 1) * wide)
            u = dot(x_c, wi[:, cols], NN)
            dz = dot(dy_c, wo[cols, :], NT)
            square = u * u
            bent = jnp.tanh(GELU_SCALE * (u + GELU_CUBE * (square * u)))
            cdf = 0.5 * (1.0 + bent)
            slope = cdf + (0.5 * GELU_SCALE) * u * (1.0 - bent * bent) * (1.0 + 3.0 * GELU_CUBE * square)
            hidden = (u * cdf).astype(BF)
            d_pre = (dz * slope).astype(BF)
            hid[rows, cols] = hidden
            dpre[rows, cols] = d_pre
            y_sum += dot(hidden, wo[cols, :], NN)
            dx_sum += dot(d_pre, wi[:, cols], NT)
        y_low = y_sum.astype(BF)
        d_gate = jnp.sum(y_low.astype(F32) * do_c, axis=1, keepdims=True)
        for n in range(per_plane):
            part = slice(n * padded, (n + 1) * padded)
            source = plane * per_plane + n
            ysend[source] = y_sum[part].astype(BF)
            dxsend[source] = dx_sum[part].astype(BF)
            dgsend[source] = jnp.sum(jnp.where(diagonal, d_gate[part], 0.0), axis=0, keepdims=True)

    def far_plane(turn):
        half = 1 - 2 * lax.rem(z, 2)
        other = lax.rem(z + 2, planes)
        return jnp.where(turn == 0, other, jnp.where(turn == 1, planes - 1 - z, z + half))

    def remote_turn(turn, carry):
        plane = far_plane(turn)
        work(plane)
        for n in range(per_plane):
            for copy in copies(plane, n):
                copy.start()
        return carry

    lax.fori_loop(0, planes - 1, remote_turn, 0)
    work(z)
    for copy in own_copies():
        copy.start()
    for n in range(per_plane):
        for copy in copies(z, n):
            pl.when(at.chip != n)(copy.start)

    @pl.when(jnp.logical_and(z >= 1, z <= 2))
    def _():
        turned = x[...].T
        for b in range(blocks):
            cols = slice(b * wide, (b + 1) * wide)
            gi[:, cols] = dot(turned, dpre[:, cols], NN, BF)
        for b in range(blocks):
            cols = slice(b * wide, (b + 1) * wide)
            go[cols, :] = dot(hid[:, cols], dy[...], TN, BF)

    def finish(step, carry):
        source = lax.rem(at.me + step, at.chips)
        plane, n = lax.div(source, per_plane), lax.rem(source, per_plane)
        rows = dxland.at[pl.ds(pl.multiple_of(source * padded, 8), padded), :]
        send_to(dxsend.at[source], rows, ts.at[0, source], tr.at[0, source], z, i).wait_recv()
        send_to(dgsend.at[source], dgland.at[source], ts.at[1, source], tr.at[1, source], z, i).wait_recv()
        for copy in copies(plane, n):
            copy.wait_send()
        return carry

    lax.fori_loop(1, at.chips, finish, 0)
    for copy in own_copies():
        copy.wait()


def mid(planes, experts, x, do, gate, win, wout):
    chips, padded, width = x.shape
    ff = win.shape[1]
    slots = chips * padded
    blocks = 4
    dma = pltpu.SemaphoreType.DMA
    vm = pltpu.VMEM
    sds = jax.ShapeDtypeStruct
    return pl.pallas_call(
        functools.partial(mid_kernel, planes, experts, padded, blocks),
        out_shape=(
            sds((chips, padded, width), BF),
            sds((width, ff), BF),
            sds((ff, width), BF),
            sds((slots, width), BF),
            sds((chips, 1, 128), F32),
        ),
        in_specs=[vmem_spec()] * 3 + [any_spec()] * 2,
        out_specs=(vmem_spec(),) * 3 + (any_spec(),) * 2,
        scratch_shapes=[
            vm((width, ff), BF),
            vm((ff, width), BF),
            vm((slots, width), BF),
            vm((slots, ff), BF),
            vm((slots, ff), BF),
            vm((chips, padded, width), BF),
            vm((chips, 1, 128), F32),
            dma((2,)), dma((2, chips)), dma((2, chips)), dma((2,)),
        ],
        compiler_params=pltpu.CompilerParams(
            collective_id=2, has_side_effects=True, vmem_limit_bytes=VMEM_LIMIT
        ),
        name="mid",
    )(x.reshape(slots, width), do.reshape(slots, width), gate, win, wout)
def back_kernel(planes, experts, capacity_rows, nrouter,
                tokens, cot, aux, ga, act_two, q, k, v, resid, probs, wd, pk,
                dx, dg, ysend, gi, go,
                block_out, grad_tokens, fb, osmall, wi, wo, yland,
                gd, dsend, ycol, dres, datt, dq, dk, dv, gsum, szb, rzb, sup, rup,
                sms, smr, small, xi, ri, xo, ro,
                ls, es, er, hs, hr, ys, yr, yl, sd, rd, us, ur, zs, zr, gs, gr, ms, mr):
    at = Place(planes, experts)
    z, i, core = at.z, at.i, at.core
    padded = capacity_rows
    chips = at.chips
    per_plane = experts // 2
    rows, width = tokens.shape
    pairs = width // 128
    spot = lax.rem(i, 8)
    base = i - spot
    upper = sup.shape[0] if experts > 8 else 0
    met = greet(at)
    ce = z - 1
    host = jnp.logical_and(z >= 1, z <= 2)
    load_i = pltpu.make_async_copy(gi.at[:, core], xi, ls.at[0])
    load_o = pltpu.make_async_copy(go.at[:, core], xo, ls.at[1])

    @pl.when(host)
    def _():
        load_i.start()
        load_o.start()

    met()
    pair_i = send_to(gi.at[:, 1 - core], ri, es.at[0], er.at[0], z, at.sib)
    pair_o = send_to(go.at[:, 1 - core], ro, es.at[1], er.at[1], z, at.sib)

    @pl.when(host)
    def _():
        pair_i.start()
        pair_o.start()

    def landing(source):
        return yland.at[pl.ds(pl.multiple_of(source * padded, 8), padded), :]

    def y_copy(step):
        target = lax.rem(at.me + step, chips)
        zt, it = lax.div(target, per_plane), 2 * lax.rem(target, per_plane) + core
        return send_to(ysend.at[target], landing(at.me), ys.at[step], yr.at[step], zt, it)

    def y_start(step, carry):
        y_copy(step).start()
        return carry

    y_own = pltpu.make_async_copy(ysend.at[at.me], landing(at.me), yl.at[0])
    y_own.start()
    lax.fori_loop(1, chips, y_start, 0)

    aux_v = aux[...]
    gates = [aux_v[:, 0:1], aux_v[:, 1:2]]
    place = slot_places([aux_v[:, 2:3], aux_v[:, 3:4]], chips * padded)
    d_out = cot[...].astype(F32)
    d_act = dot(place[0] + place[1], dx[...], NN)
    table = dg[:, 0, :]
    d_gate = slot_values(aux_v, table, padded, chips)
    mean_gate = gates[0] * d_gate[0] + gates[1] * d_gate[1]
    route_iota = lax.broadcasted_iota(jnp.int32, (rows, nrouter), 1).astype(F32)
    d_logits = jnp.zeros((rows, nrouter), F32)
    for n in range(2):
        chosen = route_iota == aux_v[:, 4 + n:5 + n]
        d_logits = d_logits + jnp.where(chosen, gates[n] * (d_gate[n] - mean_gate), 0.0)
    d_logits = d_logits.astype(BF)
    small[0:nrouter, :] = dot(d_logits, act_two[...], TN)
    d_act = d_act + dot(d_logits, pk[0:nrouter, :], NN)
    gain_one = pk[nrouter:nrouter + 1, :].astype(F32)
    gain_two = pk[nrouter + 2:nrouter + 3, :].astype(F32)
    d_norm, g_gain, g_bias = norm_back(resid[...], gain_two, d_act)
    small[nrouter:nrouter + 16, :] = jnp.zeros((16, width), F32)
    small[nrouter + 2:nrouter + 3, :] = g_gain
    small[nrouter + 3:nrouter + 4, :] = g_bias
    d_res = d_out + d_norm
    dres[...] = d_res
    d_branch = d_res.astype(BF)
    half = width // 2
    for n in range(2):
        dsend[pairs + n] = d_branch[:, n * half:(n + 1) * half]
    datt[...] = dot(d_branch, wd[3], NT, BF)

    def d_copy(target):
        return send_to(dsend.at[target], gd.at[spot], sd.at[target], rd.at[spot], z, base + target)

    def d_near(target):
        return pltpu.make_async_copy(dsend.at[target], gd.at[spot], rd.at[spot])

    def d_start(target):
        far = spot != target
        pl.when(far)(d_copy(target).start)
        pl.when(jnp.logical_not(far))(d_near(target).start)

    for n in range(2):
        d_start(pairs + n)

    owner = 2 * at.chip + ce
    shipments = []

    def ship(p, which):
        src, dst = (xi.at[p], wi.at[core]) if which == 0 else (xo.at[p], wo.at[core])
        near = jnp.logical_and(z == p, core == ce)
        far_copy = send_to(src, dst, hs.at[p, which], hr.at[core, which], p, owner)
        near_copy = pltpu.make_async_copy(src, dst, hr.at[core, which])
        is_far = jnp.logical_and(host, jnp.logical_not(near))
        pl.when(is_far)(far_copy.start)
        pl.when(jnp.logical_and(host, near))(near_copy.start)
        shipments.append((is_far, far_copy))

    def add_pair(load, pair, mine, theirs, chunk):
        @pl.when(host)
        def _():
            load.wait()
            pair.wait_recv()

            def add(n, carry):
                part = pl.ds(pl.multiple_of(n * chunk, chunk), chunk)
                for p in range(planes):
                    mine[p, part, :] = (
                        mine[p, part, :].astype(F32) + theirs[p, part, :].astype(F32)
                    ).astype(BF)
                return carry

            lax.fori_loop(0, mine.shape[1] // chunk, add, 0)

    add_pair(load_i, pair_i, xi, ri, 16)
    for p in range(planes):
        ship(p, 0)
    add_pair(load_o, pair_o, xo, ro, 64)
    for p in range(planes):
        ship(p, 1)

    lane = lax.broadcasted_iota(jnp.int32, (rows, 128), 1)
    masks = [(lane < HEAD).astype(F32).astype(BF), (lane >= HEAD).astype(F32).astype(BF)]
    score_scale = HEAD ** (-0.5)

    def head_pair(n, carry):
        cols = pl.ds(pl.multiple_of(n * 128, 128), 128)
        q2, k2, v2, da2 = q[:, cols], k[:, cols], v[:, cols], datt[:, cols]
        sums = [jnp.zeros((rows, 128), F32) for _ in range(3)]
        for side in range(2):
            mask = masks[side]
            da = da2 * mask
            p = probs[2 * n + side]
            dpb = dot(da, v2, NT)
            delta = jnp.sum(p * dpb, axis=-1, keepdims=True)
            ds = (p * (dpb - delta)).astype(BF)
            sums[0] += dot(ds, k2 * mask, NN)
            sums[1] += dot(ds, q2 * mask, TN)
            sums[2] += dot(p.astype(BF), da, TN)
        low = [(sums[0] * score_scale).astype(BF), (sums[1] * score_scale).astype(BF), sums[2].astype(BF)]
        for m, (value, full) in enumerate(zip(low, (dq, dk, dv))):
            dsend[n, :, m * 128:(m + 1) * 128] = value
            full[:, cols] = value
        d_start(n)
        return carry

    lax.fori_loop(0, pairs, head_pair, 0)

    d_one = dot(dq[...], wd[0], NT) + dot(dk[...], wd[1], NT) + dot(dv[...], wd[2], NT)
    d_norm, g_gain, g_bias = norm_back(tokens[...].astype(F32), gain_one, d_one)
    grad_tokens[...] = (dres[...] + d_norm).astype(BF)
    small[nrouter:nrouter + 1, :] = g_gain
    small[nrouter + 1:nrouter + 2, :] = g_bias

    hops = [at.sib, at.xn, at.yn]
    for n in range(upper):
        bit = 8 << n
        hops.append(i + bit - 2 * bit * lax.rem(lax.div(i, bit), 2))
    moves = [(z, t) for t in hops]
    for n in range(planes.bit_length() - 1):
        bit = 1 << n
        moves.append((z + bit - 2 * bit * lax.rem(lax.div(z, bit), 2), i))
    small_copies = []

    def small_start(n):
        sms[n] = small[...]
        copy = send_to(sms.at[n], smr.at[n], ms.at[n], mr.at[n], moves[n][0], moves[n][1])
        copy.start()
        small_copies.append(copy)

    def small_step(n):
        small_copies[n].wait_recv()
        small[...] = small[...] + smr[n]
        if n + 1 < len(moves):
            small_start(n + 1)

    small_start(0)

    small_step(0)

    def d_wait(source, carry):
        send_to(gd.at[source], gd.at[source], sd.at[source], rd.at[source], z, i).wait_recv()
        return carry

    lax.fori_loop(0, 8, d_wait, 0)
    columns = gd.shape[2]
    total = dot(ga[...].reshape(8 * rows, width), gd[...].reshape(8 * rows, columns), TN)
    gsum[...] = total.reshape(planes, width // planes, columns)
    small_step(1)
    tail = []
    for n in range(upper):
        sup[n] = gsum[...].astype(BF)
        copy = send_to(sup.at[n], rup.at[n], us.at[n], ur.at[n], z, hops[3 + n])
        copy.start()
        tail.append(copy)
        copy.wait_recv()
        gsum[...] = sup[n].astype(F32) + rup[n].astype(F32)
    szb[...] = gsum[...].astype(BF)
    for j in range(1, planes):
        zt = lax.rem(z + j, planes)
        copy = send_to(szb.at[zt], rzb.at[j - 1], zs.at[j - 1], zr.at[j - 1], zt, i)
        copy.start()
        tail.append(copy)
    small_step(2)

    def y_finish(step, carry):
        source = lax.rem(at.me + chips - step, chips)
        send_to(landing(source), landing(source), ys.at[step], yr.at[step], z, i).wait_recv()
        y_copy(step).wait_send()
        return carry

    y_own.wait()
    lax.fori_loop(1, chips, y_finish, 0)
    fetch = pltpu.make_async_copy(yland, ycol, yl.at[1])
    fetch.start()
    fetch.wait()
    y_all = ycol[...]
    mixed = gates[0] * dot(place[0], y_all, NN) + gates[1] * dot(place[1], y_all, NN)
    block_out[...] = (resid[...] + mixed).astype(BF)

    fin = gsum[z]
    for j in range(1, planes):
        send_to(rzb.at[j - 1], rzb.at[j - 1], zs.at[j - 1], zr.at[j - 1], z, i).wait_recv()
        fin = fin + rzb[j - 1].astype(F32)
    fb[spot] = fin.astype(BF)
    px, py = spot + 2 - 4 * at.xb, spot + 4 - 8 * at.yb
    pd = px + 4 - 8 * at.yb
    flip = 1 - 2 * core

    def pass_on(where, step, target):
        copy = send_to(fb.at[where], fb.at[where], gs.at[step], gr.at[step], z, target)
        copy.start()
        tail.append(copy)

    def landed(where, step):
        send_to(fb.at[where], fb.at[where], gs.at[step], gr.at[step], z, i).wait_recv()

    pass_on(spot, 0, at.xn)
    pass_on(spot, 1, at.yn)
    pass_on(spot, 2, at.sib)
    small_step(3)
    landed(px, 0)
    landed(py, 1)
    pass_on(px + core * (py - px), 3, at.yn + core * (at.xn - at.yn))
    pass_on(px, 4, at.sib)
    pass_on(py, 5, at.sib)
    for n in range(4, len(moves)):
        small_step(n)
    osmall[...] = small[...]
    landed(pd, 3)
    pass_on(pd, 6, at.sib)
    for h in range(2):
        send_to(wi.at[h], wi.at[h], hs.at[0, 0], hr.at[h, 0], z, i).wait_recv()
        send_to(wo.at[h], wo.at[h], hs.at[0, 1], hr.at[h, 1], z, i).wait_recv()
    landed(spot + flip, 2)
    landed(px + flip, 4)
    landed(py + flip, 5)
    landed(pd + flip, 6)
    for copy in tail + small_copies:
        copy.wait_send()
    def d_sent(target, carry):
        pl.when(spot != target)(d_copy(target).wait_send)
        return carry

    lax.fori_loop(0, 8, d_sent, 0)

    @pl.when(host)
    def _():
        pair_i.wait_send()
        pair_o.wait_send()

    for is_far, copy in shipments:
        pl.when(is_far)(copy.wait_send)


def back(planes, experts, nrouter, tokens, cot, aux, ga, act_two, q, k, v, resid,
         probs, wd, pk, dx, dg, ysend, gi, go):
    rows, width = tokens.shape
    chips, padded, _ = ysend.shape
    ff = gi.shape[1]
    share, fshare, half = width // planes, ff // planes, width // 2
    upper = max(experts.bit_length() - 4, 1)
    nbits = experts.bit_length() - 1 + planes.bit_length() - 1
    gi = gi.reshape(planes, 2, share // 2, ff)
    go = go.reshape(planes, 2, fshare // 2, width)
    dma = pltpu.SemaphoreType.DMA
    vm = pltpu.VMEM
    sds = jax.ShapeDtypeStruct
    return pl.pallas_call(
        functools.partial(back_kernel, planes, experts, padded, nrouter),
        out_shape=(
            sds((rows, width), BF),
            sds((rows, width), BF),
                    sds((8, share, half), BF),
            sds((nrouter + 16, width), F32),
            sds((2, share // 2, ff), BF),
            sds((2, fshare // 2, width), BF),
            sds((chips * padded, width), BF),
        ),
        in_specs=[vmem_spec()] * 15 + [any_spec()] * 2,
        out_specs=(vmem_spec(),) * 6 + (any_spec(),),
        scratch_shapes=[
            vm((8, rows, half), BF),
            vm((8, rows, half), BF),
            vm((chips * padded, width), BF),
            vm((rows, width), F32),
            vm((rows, width), BF),
            vm((rows, width), BF),
            vm((rows, width), BF),
            vm((rows, width), BF),
            vm((planes, share, half), F32),
            vm((planes, share, half), BF),
            vm((planes - 1, share, half), BF),
            vm((upper, planes, share, half), BF),
            vm((upper, planes, share, half), BF),
            vm((nbits, nrouter + 16, width), F32),
            vm((nbits, nrouter + 16, width), F32),
            vm((nrouter + 16, width), F32),
            vm((planes, share // 2, ff), BF),
            vm((planes, share // 2, ff), BF),
            vm((planes, fshare // 2, width), BF),
            vm((planes, fshare // 2, width), BF),
            dma((2,)), dma((2,)), dma((2,)),
            dma((planes, 2)), dma((2, 2)),
            dma((chips,)), dma((chips,)), dma((2,)),
            dma((8,)), dma((8,)),
            dma((upper,)), dma((upper,)),
            dma((planes - 1,)), dma((planes - 1,)),
            dma((7,)), dma((7,)), dma((nbits,)), dma((nbits,)),
        ],
        compiler_params=pltpu.CompilerParams(
            collective_id=3, has_side_effects=True, vmem_limit_bytes=VMEM_LIMIT
        ),
        name="back",
    )(tokens, cot, aux, ga, act_two, q, k, v, resid, probs, wd, pk, dx, dg, ysend, gi, go)


def finish_kernel(planes, nrouter, block_out, grad_tokens, fb, small, wi, wo,
                  ob, ot, o0, o1, o2, o3, og, ov, ogi, ogo,
                  s0, s1, s2, s3, sg, sv, si, so, sem):
    z = lax.axis_index("dp")
    share = s0.shape[0]
    pairs = s0.shape[1] // 128
    half = s0.shape[1] // 2
    copies = []

    def write(source, target):
        copy = pltpu.make_async_copy(source, target, sem.at[len(copies)])
        copy.start()
        copies.append(copy)

    write(block_out, ob)
    write(grad_tokens, ot)
    for wide, low, out in ((si, wi, ogi), (so, wo, ogo)):
        chunk = low.shape[1]
        for h in range(2):
            wide[h * chunk:(h + 1) * chunk, :] = low[h].astype(F32)
            write(wide.at[pl.ds(h * chunk, chunk), :], out.at[pl.ds(h * chunk, chunk), :])
    for m, (stage, out) in enumerate(((s0, o0), (s1, o1), (s2, o2))):
        for n in range(pairs):
            stage[:, n * 128:(n + 1) * 128] = fb[n, :, m * 128:(m + 1) * 128].astype(F32)
        write(stage, out)
    for n in range(2):
        s3[:, n * half:(n + 1) * half] = fb[pairs + n].astype(F32)
    write(s3, o3)
    mine = small[:, 0:share]
    for p in range(1, planes):
        mine = jnp.where(z == p, small[:, p * share:(p + 1) * share], mine)
    sg[...] = mine[0:nrouter]
    write(sg, og)
    for n in range(4):
        sv[n] = mine[nrouter + n:nrouter + n + 1]
        write(sv.at[n], ov.at[n])
    for copy in copies:
        copy.wait()


def finish(planes, nrouter, block_out, grad_tokens, fb, small, wi, wo):
    rows, width = block_out.shape
    _, share, half = fb.shape
    ff = wi.shape[2]
    fshare = 2 * wo.shape[1]
    vm = pltpu.VMEM
    sds = jax.ShapeDtypeStruct
    flat = ((share, width),) * 4 + ((nrouter, share), (4, 1, share), (share, ff), (fshare, width))
    return pl.pallas_call(
        functools.partial(finish_kernel, planes, nrouter),
        out_shape=(sds((rows, width), BF),) * 2 + tuple(sds(shape, F32) for shape in flat),
        in_specs=[vmem_spec()] * 6,
        out_specs=(any_spec(),) * 10,
        scratch_shapes=[vm(shape, F32) for shape in flat] + [pltpu.SemaphoreType.DMA((16,))],
        compiler_params=pltpu.CompilerParams(vmem_limit_bytes=VMEM_LIMIT),
        name="finish",
    )(block_out, grad_tokens, fb, small, wi, wo)


def shards(planes, experts, tokens, segment_ids, routes, ln1_gain, ln1_bias, ln2_gain, ln2_bias,
           w_query, w_key, w_value, w_output, w_router, frozen_in, frozen_out, new_in, new_out,
           cotangent):
    rows, width = tokens.shape
    expert_count = w_router.shape[1]
    capacity = 5 * rows // (2 * expert_count)
    padded = -(-capacity // 8) * 8
    (wd, pk, win, wout, _, act_two, q, k, v, _, resid, probs, aux, ga, x_recv, do_recv, g_recv) = front(
        planes, experts, capacity, padded, expert_count, tokens, cotangent, segment_ids, routes,
        w_router, (ln1_gain, ln1_bias, ln2_gain, ln2_bias),
        w_query, w_key, w_value, w_output, frozen_in, frozen_out, new_in, new_out,
    )
    y_rows, grad_in, grad_out, dx_back, dg_back = mid(
        planes, experts, x_recv, do_recv, g_recv, win, wout
    )
    block_out, grad_tokens, dense, small, low_in, low_out, _ = back(
        planes, experts, expert_count, tokens, cotangent, aux, ga, act_two, q, k, v,
        resid, probs, wd, pk, dx_back, dg_back, y_rows, grad_in, grad_out,
    )
    block_out, grad_tokens, oq, ok, ov, ow, router, norms, ogi, ogo = finish(
        planes, expert_count, block_out, grad_tokens, dense, small, low_in, low_out
    )
    norms = norms.reshape(4, width // planes)
    return (
        block_out, grad_tokens, oq, ok, ov, ow, router.T,
        norms[0], norms[1], norms[2], norms[3], ogi[None], ogo[None],
    )


def solution(mesh):
    rows = P(("dp", "expert"), None)
    in_specs = (rows, rows, rows) + (P("dp"),) * 4 + (P("dp", None),) * 5
    in_specs += (P("expert", "dp", None),) * 4 + (rows,)
    out_specs = (rows, rows) + (P("dp", None),) * 5 + (P("dp"),) * 4
    out_specs += (P("expert", "dp", None),) * 2
    body = functools.partial(shards, mesh.shape["dp"], mesh.shape["expert"])
    return jax.shard_map(body, mesh=mesh, in_specs=in_specs, out_specs=out_specs, check_vma=False)
```

time: 1030 us -> 330 us (0.32)
  waiting for transfers between devices: 702 us -> 0 us
  Pallas kernels: 0 us -> 324 us
  blocking collectives: 104 us -> 0 us
  matrix products: 91.2 us -> 0 us
  local copies, waits for them, and re-layouts: 60.8 us -> 1.26 us
  other arithmetic: 40.4 us -> 0 us
  between operations: 16.2 us -> 0.68 us
    all_gather x8 -> x0, waiting for transfers between devices: 408 us -> none  [the longest x1 89.8 us: shards(): lax.all_gather(new_in[0].astype(jnp.bfloat16), 'dp', axis=0, tiled=True)]
    pallas_call x0 -> x4, Pallas kernels: none -> 324 us  [the longest x1 174 us: front(): pl.pallas_call(functools.partial(front_kernel, planes, experts, capacity,...]
    reduce_scatter x2 -> x0, waiting for transfers between devices: 165 us -> none  [the longest x1 85.2 us: shards(): lax.psum_scatter(grad_out_full.astype(jnp.bfloat16), 'dp', scatter_dimens...]
    psum x1 -> x0, waiting for transfers between devices: 123 us -> none  [shards(): lax.psum((grad_query, grad_key, grad_value, grad_output, grad_router, gra...]
    dot_general x27 -> x0, matrix products: 91.2 us -> none  [the longest x1 12.5 us: shards(): jnp.einsum('sekd,efd->sekf', d_produced, back_out, preferred_element_type...]
    psum x1 -> x0, blocking collectives: 38.8 us -> none  [shards(): lax.psum((grad_query, grad_key, grad_value, grad_output, grad_router, gra...]
    all_to_all x2 -> x0, blocking collectives: 37.6 us -> none  [the longest x1 19.1 us: shards(): lax.all_to_all(d_send, 'expert', split_axis=0, concat_axis=0, tiled=True)]
    gather x5 -> x0, local copies, waits for them, and re-layouts: 16.7 us -> none  [the longest x1 4.61 us: shards(): jnp.concatenate([pair_weight, jnp.zeros((1,), jnp.float32)])[pair_of_slot]]
  transfers between devices with their start and end apart: 13 -> 0, of which waited for: 11 -> 0; matrix products, arithmetic and copies ran while one was open for 9% -> 0% of each run, Pallas kernels for 0% -> 0%
where the time goes in v1:
time: 330 us; the launch traced here: 326 us
  Pallas kernels  324 us (98%)
    pallas_call x1, Pallas kernels, front(): pl.pallas_call(functools.partial(front_kernel, planes, experts, capacity,...  174 us
    pallas_call x1, Pallas kernels, back(): pl.pallas_call(functools.partial(back_kernel, planes, experts, padded, nr...  109 us
    pallas_call x1, Pallas kernels, mid(): pl.pallas_call(functools.partial(mid_kernel, planes, experts, padded, blo...  35.7 us

profile of v1, /device:TPU:0, one launch (start us, length us, event | category | flops | bytes accessed | tf_op | source)
XLA Modules:
  0.0 325.7 jit_solution(15305985675146962882)
XLA Ops:
  0.7 173.7 %front.1 = (bf16[4,768,768]{2,1,0:T(8,128)(2,1)}, bf16[32,768]{1,0:T(8,128)(2,1)}, bf16[768,3072]{1,0:T(8,128)(2,1)}, bf16[3072,768]{1,0:T(8,128)(2,1)}, bf16[25...) custom-call(bf16[256,768]{1,0:T(8,128)(2,1)} %tokens.3, ...), custom_call_target="tpu_custom_call" | custom-call | tf_op jit(solution)/shard_map/front/pallas_call | solution.py:453
  174.4 35.7 %mid.1 = (bf16[16,40,768]{2,1,0:T(8,128)(2,1)}, bf16[768,3072]{1,0:T(8,128)(2,1)}, bf16[3072,768]{1,0:T(8,128)(2,1)}, bf16[640,768]{1,0:T(8,128)(2,1)}, f32[16,1,128]{2,1,0:T(1,128)}) custom-call(bf16[640,768]{1,0:T(8,128)(2,1)} %bitcast.19, bf16[640,768]{1,0:T(8,128)(2,1)} %bitcast.20, f32[16,1,128]{2,1,0:T(1,128)} %get-tuple-element.61.gate, ...), custom_call_target="tpu_custom_call" | custom-call | tf_op jit(solution)/shard_map/mid/pallas_call | solution.py:631
  210.1 108.7 %back.1 = (bf16[256,768]{1,0:T(8,128)(2,1)}, bf16[256,768]{1,0:T(8,128)(2,1)}, bf16[8,192,384]{2,1,0:T(8,128)(2,1)}, f32[32,768]{1,0:T(8,128)}, bf16[2,96,3072]{...) custom-call(bf16[256,768]{1,0:T(8,128)(2,1)} %tokens.3, bf16[256,768]{1,0:T(8,128)(2,1)} %cot.3, ...), custom_call_target="tpu_custom_call" | custom-call | tf_op jit(solution)/shard_map/back/pallas_call | solution.py:957
  318.9 5.6 %finish.1 = (bf16[256,768]{1,0:T(8,128)(2,1)}, bf16[256,768]{1,0:T(8,128)(2,1)}, f32[192,768]{1,0:T(8,128)}, f32[192,768]{1,0:T(8,128)}, f32[192,768]{1,0:T(8,12...) custom-call(bf16[256,768]{1,0:T(8,128)(2,1)} %get-tuple-element.69.b, ...), custom_call_target="tpu_custom_call" | custom-call | tf_op jit(solution)/shard_map/finish/pallas_call | solution.py:1054
  324.4 1.3 fusion

commit v2 on v1

--- a/solution.py
+++ b/solution.py
@@ -15,6 +15,7 @@
 BF = jnp.bfloat16
 F32 = jnp.float32
 VMEM_LIMIT = 60 * 1024 * 1024
+REAR_LIMIT = 67043328
 
 
 class Place:
@@ -497,25 +498,35 @@
 GELU_CUBE = 0.044715
 
 
-def mid_kernel(planes, experts, padded, blocks,
-               x, do, gate, win, wout,
-               ysend, gi, go, dxland, dgland,
-               wi, wo, dy, hid, dpre, dxsend, dgsend,
-               ls, ts, tr, tl):
+def rear_kernel(planes, experts, padded, pieces, blocks, ga_groups, nrouter,
+                x, do, gate, tokens, cot, aux, act_two, q, k, v, resid, probs, wd, pk, win, wout, ga,
+                block_out, grad_tokens, fb, osmall, wi, wo, yland, dxland,
+                hwi, hwo, dy, hid, dpre, dxsend, dgsend, dgland, ysend, landed_rows,
+                gd, dsend, dres, gsum, szb, rzb, rup,
+                sms, smr, small, ri, ro,
+                ls, ts, tr, tl, gl,
+                es, er, hs, hr, ys, yr, yl, sd, rd, us, ur, zs, zr, gs, gr, ms, mr):
     at = Place(planes, experts)
     z, i, core = at.z, at.i, at.core
+    chips = at.chips
     per_plane = experts // 2
-    chunk = per_plane * padded
-    width = x.shape[1]
-    ff = wi.shape[1]
+    rows, width = tokens.shape
+    pairs = width // 128
+    spot = lax.rem(i, 8)
+    base = i - spot
+    upper = rup.shape[0] if experts > 8 else 0
+    ga_rows = 8 * rows // ga_groups
+    datt, dq, dk, dv = [dpre.at[pl.ds(0, rows), pl.ds(n * width, width)] for n in range(4)]
+    chunk = per_plane * padded // pieces
+    batch = per_plane // pieces
+    ff = hwi.shape[1]
     wide = ff // blocks
-    load_i = pltpu.make_async_copy(win, wi, ls.at[0])
-    load_o = pltpu.make_async_copy(wout, wo, ls.at[1])
+    load_i = pltpu.make_async_copy(win, hwi, ls.at[0])
+    load_o = pltpu.make_async_copy(wout, hwo, ls.at[1])
     load_i.start()
     load_o.start()
     met = greet(at)
-    lane = lax.broadcasted_iota(jnp.int32, (padded, 128), 1)
-    diagonal = lane == lax.broadcasted_iota(jnp.int32, (padded, 128), 0)
+    diagonal = lax.broadcasted_iota(jnp.int32, (padded, 128), 1) == lax.broadcasted_iota(jnp.int32, (padded, 128), 0)
     load_i.wait()
     load_o.wait()
     met()
@@ -523,53 +534,54 @@
     def copies(plane, n):
         target = plane * per_plane + n
         there = 2 * n + core
-        rows = dxland.at[pl.ds(pl.multiple_of(at.me * padded, 8), padded), :]
+        rows_in = dxland.at[pl.ds(pl.multiple_of(at.me * padded, 8), padded), :]
         return [
-            send_to(dxsend.at[target], rows, ts.at[0, target], tr.at[0, at.me], plane, there),
+            send_to(dxsend.at[target], rows_in, ts.at[0, target], tr.at[0, at.me], plane, there),
             send_to(dgsend.at[target], dgland.at[at.me], ts.at[1, target], tr.at[1, at.me], plane, there),
         ]
 
     def own_copies():
-        rows = dxland.at[pl.ds(pl.multiple_of(at.me * padded, 8), padded), :]
+        rows_in = dxland.at[pl.ds(pl.multiple_of(at.me * padded, 8), padded), :]
         return [
-            pltpu.make_async_copy(dxsend.at[at.me], rows, tl.at[0]),
+            pltpu.make_async_copy(dxsend.at[at.me], rows_in, tl.at[0]),
             pltpu.make_async_copy(dgsend.at[at.me], dgland.at[at.me], tl.at[1]),
         ]
 
-    def work(plane):
-        rows = pl.ds(pl.multiple_of(plane * chunk, 16), chunk)
-        x_c = x[rows, :]
-        do_c = do[rows, :].astype(F32)
+    def work(plane, piece):
+        first = plane * per_plane + piece * batch
+        span = pl.ds(pl.multiple_of((plane * pieces + piece) * chunk, 16), chunk)
+        x_c = x[span, :]
+        do_c = do[span, :].astype(F32)
         column = jnp.concatenate(
             [
-                jnp.sum(jnp.where(diagonal, gate[plane * per_plane + n], 0.0), axis=1, keepdims=True)
-                for n in range(per_plane)
+                jnp.sum(jnp.where(diagonal, gate[first + n], 0.0), axis=1, keepdims=True)
+                for n in range(batch)
             ],
             axis=0,
         )
         dy_c = (do_c * column).astype(BF)
-        dy[rows, :] = dy_c
+        dy[span, :] = dy_c
         y_sum = jnp.zeros((chunk, width), F32)
         dx_sum = jnp.zeros((chunk, width), F32)
         for b in range(blocks):
             cols = slice(b * wide, (b + 1) * wide)
-            u = dot(x_c, wi[:, cols], NN)
-            dz = dot(dy_c, wo[cols, :], NT)
+            u = dot(x_c, hwi[:, cols], NN)
+            dz = dot(dy_c, hwo[cols, :], NT)
             square = u * u
             bent = jnp.tanh(GELU_SCALE * (u + GELU_CUBE * (square * u)))
             cdf = 0.5 * (1.0 + bent)
             slope = cdf + (0.5 * GELU_SCALE) * u * (1.0 - bent * bent) * (1.0 + 3.0 * GELU_CUBE * square)
             hidden = (u * cdf).astype(BF)
             d_pre = (dz * slope).astype(BF)
-            hid[rows, cols] = hidden
-            dpre[rows, cols] = d_pre
-            y_sum += dot(hidden, wo[cols, :], NN)
-            dx_sum += dot(d_pre, wi[:, cols], NT)
+            hid[span, cols] = hidden
+            dpre[span, cols] = d_pre
+            y_sum += dot(hidden, hwo[cols, :], NN)
+            dx_sum += dot(d_pre, hwi[:, cols], NT)
         y_low = y_sum.astype(BF)
         d_gate = jnp.sum(y_low.astype(F32) * do_c, axis=1, keepdims=True)
-        for n in range(per_plane):
+        for n in range(batch):
             part = slice(n * padded, (n + 1) * padded)
-            source = plane * per_plane + n
+            source = first + n
             ysend[source] = y_sum[part].astype(BF)
             dxsend[source] = dx_sum[part].astype(BF)
             dgsend[source] = jnp.sum(jnp.where(diagonal, d_gate[part], 0.0), axis=0, keepdims=True)
@@ -580,139 +592,99 @@
         return jnp.where(turn == 0, other, jnp.where(turn == 1, planes - 1 - z, z + half))
 
     def remote_turn(turn, carry):
-        plane = far_plane(turn)
-        work(plane)
-        for n in range(per_plane):
-            for copy in copies(plane, n):
+        plane = far_plane(lax.div(turn, pieces))
+        piece = lax.rem(turn, pieces)
+        work(plane, piece)
+        for n in range(batch):
+            for copy in copies(plane, piece * batch + n):
                 copy.start()
         return carry
 
-    lax.fori_loop(0, planes - 1, remote_turn, 0)
-    work(z)
+    lax.fori_loop(0, (planes - 1) * pieces, remote_turn, 0)
+    for piece in range(pieces):
+        work(z, piece)
     for copy in own_copies():
         copy.start()
     for n in range(per_plane):
         for copy in copies(z, n):
             pl.when(at.chip != n)(copy.start)
 
-    @pl.when(jnp.logical_and(z >= 1, z <= 2))
+    def landing(source):
+        return yland.at[pl.ds(pl.multiple_of(source * padded, 8), padded), :]
+
+    def y_copy(step):
+        target = lax.rem(at.me + step, chips)
+        zt, it = lax.div(target, per_plane), 2 * lax.rem(target, per_plane) + core
+        return send_to(ysend.at[target], landing(at.me), ys.at[step], yr.at[step], zt, it)
+
+    def y_start(step, carry):
+        y_copy(step).start()
+        return carry
+
+    y_own = pltpu.make_async_copy(ysend.at[at.me], landing(at.me), yl.at[0])
+    y_own.start()
+    lax.fori_loop(1, chips, y_start, 0)
+
+    ce = z - 1
+    host = jnp.logical_and(z >= 1, z <= 2)
+    half_i, half_o = width // planes // 2, ff // planes // 2
+
+    def part(source, size, p, c):
+        return source.at[pl.ds(pl.multiple_of((2 * p + c) * size, 16), size), :]
+
+    pair = [
+        [
+            send_to(part(src, size, p, 1 - core), land.at[p], es.at[which, p], er.at[which, p], z, at.sib)
+            for p in range(planes)
+        ]
+        for which, (src, land, size) in enumerate(((hwi, ri, half_i), (hwo, ro, half_o)))
+    ]
+    fetch_ga = [
+        pltpu.make_async_copy(
+            ga.at[pl.ds(g * ga_rows, ga_rows), :],
+            hid.at[pl.ds(0, ga_rows), pl.ds(g * width, width)],
+            gl.at[g],
+        )
+        for g in range(ga_groups)
+    ]
+
+    @pl.when(host)
     def _():
         turned = x[...].T
         for b in range(blocks):
             cols = slice(b * wide, (b + 1) * wide)
-            gi[:, cols] = dot(turned, dpre[:, cols], NN, BF)
+            hwi[:, cols] = dot(turned, dpre[:, cols], NN, BF)
+        for copy in pair[0]:
+            copy.start()
         for b in range(blocks):
             cols = slice(b * wide, (b + 1) * wide)
-            go[cols, :] = dot(hid[:, cols], dy[...], TN, BF)
-
-    def finish(step, carry):
+            hwo[cols, :] = dot(hid[:, cols], dy[...], TN, BF)
+        for copy in pair[1]:
+            copy.start()
+
+    for copy in fetch_ga:
+        copy.start()
+
+    def dx_wait(step, carry):
         source = lax.rem(at.me + step, at.chips)
-        plane, n = lax.div(source, per_plane), lax.rem(source, per_plane)
-        rows = dxland.at[pl.ds(pl.multiple_of(source * padded, 8), padded), :]
-        send_to(dxsend.at[source], rows, ts.at[0, source], tr.at[0, source], z, i).wait_recv()
+        rows_in = dxland.at[pl.ds(pl.multiple_of(source * padded, 8), padded), :]
+        send_to(dxsend.at[source], rows_in, ts.at[0, source], tr.at[0, source], z, i).wait_recv()
         send_to(dgsend.at[source], dgland.at[source], ts.at[1, source], tr.at[1, source], z, i).wait_recv()
-        for copy in copies(plane, n):
-            copy.wait_send()
         return carry
 
-    lax.fori_loop(1, at.chips, finish, 0)
     for copy in own_copies():
         copy.wait()
-
-
-def mid(planes, experts, x, do, gate, win, wout):
-    chips, padded, width = x.shape
-    ff = win.shape[1]
-    slots = chips * padded
-    blocks = 4
-    dma = pltpu.SemaphoreType.DMA
-    vm = pltpu.VMEM
-    sds = jax.ShapeDtypeStruct
-    return pl.pallas_call(
-        functools.partial(mid_kernel, planes, experts, padded, blocks),
-        out_shape=(
-            sds((chips, padded, width), BF),
-            sds((width, ff), BF),
-            sds((ff, width), BF),
-            sds((slots, width), BF),
-            sds((chips, 1, 128), F32),
-        ),
-        in_specs=[vmem_spec()] * 3 + [any_spec()] * 2,
-        out_specs=(vmem_spec(),) * 3 + (any_spec(),) * 2,
-        scratch_shapes=[
-            vm((width, ff), BF),
-            vm((ff, width), BF),
-            vm((slots, width), BF),
-            vm((slots, ff), BF),
-            vm((slots, ff), BF),
-            vm((chips, padded, width), BF),
-            vm((chips, 1, 128), F32),
-            dma((2,)), dma((2, chips)), dma((2, chips)), dma((2,)),
-        ],
-        compiler_params=pltpu.CompilerParams(
-            collective_id=2, has_side_effects=True, vmem_limit_bytes=VMEM_LIMIT
-        ),
-        name="mid",
-    )(x.reshape(slots, width), do.reshape(slots, width), gate, win, wout)
-def back_kernel(planes, experts, capacity_rows, nrouter,
-                tokens, cot, aux, ga, act_two, q, k, v, resid, probs, wd, pk,
-                dx, dg, ysend, gi, go,
-                block_out, grad_tokens, fb, osmall, wi, wo, yland,
-                gd, dsend, ycol, dres, datt, dq, dk, dv, gsum, szb, rzb, sup, rup,
-                sms, smr, small, xi, ri, xo, ro,
-                ls, es, er, hs, hr, ys, yr, yl, sd, rd, us, ur, zs, zr, gs, gr, ms, mr):
-    at = Place(planes, experts)
-    z, i, core = at.z, at.i, at.core
-    padded = capacity_rows
-    chips = at.chips
-    per_plane = experts // 2
-    rows, width = tokens.shape
-    pairs = width // 128
-    spot = lax.rem(i, 8)
-    base = i - spot
-    upper = sup.shape[0] if experts > 8 else 0
-    met = greet(at)
-    ce = z - 1
-    host = jnp.logical_and(z >= 1, z <= 2)
-    load_i = pltpu.make_async_copy(gi.at[:, core], xi, ls.at[0])
-    load_o = pltpu.make_async_copy(go.at[:, core], xo, ls.at[1])
-
-    @pl.when(host)
-    def _():
-        load_i.start()
-        load_o.start()
-
-    met()
-    pair_i = send_to(gi.at[:, 1 - core], ri, es.at[0], er.at[0], z, at.sib)
-    pair_o = send_to(go.at[:, 1 - core], ro, es.at[1], er.at[1], z, at.sib)
-
-    @pl.when(host)
-    def _():
-        pair_i.start()
-        pair_o.start()
-
-    def landing(source):
-        return yland.at[pl.ds(pl.multiple_of(source * padded, 8), padded), :]
-
-    def y_copy(step):
-        target = lax.rem(at.me + step, chips)
-        zt, it = lax.div(target, per_plane), 2 * lax.rem(target, per_plane) + core
-        return send_to(ysend.at[target], landing(at.me), ys.at[step], yr.at[step], zt, it)
-
-    def y_start(step, carry):
-        y_copy(step).start()
-        return carry
-
-    y_own = pltpu.make_async_copy(ysend.at[at.me], landing(at.me), yl.at[0])
-    y_own.start()
-    lax.fori_loop(1, chips, y_start, 0)
+    lax.fori_loop(1, at.chips, dx_wait, 0)
+    fetch_dx = pltpu.make_async_copy(dxland, landed_rows, yl.at[1])
+    fetch_dx.start()
+    fetch_dx.wait()
 
     aux_v = aux[...]
     gates = [aux_v[:, 0:1], aux_v[:, 1:2]]
     place = slot_places([aux_v[:, 2:3], aux_v[:, 3:4]], chips * padded)
     d_out = cot[...].astype(F32)
-    d_act = dot(place[0] + place[1], dx[...], NN)
-    table = dg[:, 0, :]
+    d_act = dot(place[0] + place[1], landed_rows[...], NN)
+    table = dgland[:, 0, :]
     d_gate = slot_values(aux_v, table, padded, chips)
     mean_gate = gates[0] * d_gate[0] + gates[1] * d_gate[1]
     route_iota = lax.broadcasted_iota(jnp.int32, (rows, nrouter), 1).astype(F32)
@@ -755,7 +727,7 @@
     shipments = []
 
     def ship(p, which):
-        src, dst = (xi.at[p], wi.at[core]) if which == 0 else (xo.at[p], wo.at[core])
+        src, dst = (part(hwi, half_i, p, core), wi.at[core]) if which == 0 else (part(hwo, half_o, p, core), wo.at[core])
         near = jnp.logical_and(z == p, core == ce)
         far_copy = send_to(src, dst, hs.at[p, which], hr.at[core, which], p, owner)
         near_copy = pltpu.make_async_copy(src, dst, hr.at[core, which])
@@ -764,28 +736,26 @@
         pl.when(jnp.logical_and(host, near))(near_copy.start)
         shipments.append((is_far, far_copy))
 
-    def add_pair(load, pair, mine, theirs, chunk):
+    def add_pair(which, mine, theirs, size, chunk):
         @pl.when(host)
         def _():
-            load.wait()
-            pair.wait_recv()
+            for copy in pair[which]:
+                copy.wait_recv()
 
             def add(n, carry):
-                part = pl.ds(pl.multiple_of(n * chunk, chunk), chunk)
+                low = pl.ds(pl.multiple_of(n * chunk, chunk), chunk)
                 for p in range(planes):
-                    mine[p, part, :] = (
-                        mine[p, part, :].astype(F32) + theirs[p, part, :].astype(F32)
+                    here = pl.ds(pl.multiple_of((2 * p + core) * size + n * chunk, 16), chunk)
+                    mine[here, :] = (
+                        mine[here, :].astype(F32) + theirs[p, low, :].astype(F32)
                     ).astype(BF)
                 return carry
 
-            lax.fori_loop(0, mine.shape[1] // chunk, add, 0)
-
-    add_pair(load_i, pair_i, xi, ri, 16)
+            lax.fori_loop(0, size // chunk, add, 0)
+
+    add_pair(0, hwi, ri, half_i, 16)
     for p in range(planes):
         ship(p, 0)
-    add_pair(load_o, pair_o, xo, ro, 64)
-    for p in range(planes):
-        ship(p, 1)
 
     lane = lax.broadcasted_iota(jnp.int32, (rows, 128), 1)
     masks = [(lane < HEAD).astype(F32).astype(BF), (lane >= HEAD).astype(F32).astype(BF)]
@@ -831,8 +801,10 @@
     small_copies = []
 
     def small_start(n):
-        sms[n] = small[...]
-        copy = send_to(sms.at[n], smr.at[n], ms.at[n], mr.at[n], moves[n][0], moves[n][1])
+        if n >= 2:
+            small_copies[n - 2].wait_send()
+        sms[n % 2] = small[...]
+        copy = send_to(sms.at[n % 2], smr.at[n], ms.at[n], mr.at[n], moves[n][0], moves[n][1])
         copy.start()
         small_copies.append(copy)
 
@@ -843,6 +815,7 @@
             small_start(n + 1)
 
     small_start(0)
+    add_pair(1, hwo, ro, half_o, 64)
 
     small_step(0)
 
@@ -852,23 +825,32 @@
 
     lax.fori_loop(0, 8, d_wait, 0)
     columns = gd.shape[2]
-    total = dot(ga[...].reshape(8 * rows, width), gd[...].reshape(8 * rows, columns), TN)
+    total = jnp.zeros((width, columns), F32)
+    sources = ga_rows // rows
+    for g in range(ga_groups):
+        fetch_ga[g].wait()
+        total += dot(
+            hid[0:ga_rows, g * width:(g + 1) * width],
+            gd[g * sources:(g + 1) * sources].reshape(ga_rows, columns), TN,
+        )
     gsum[...] = total.reshape(planes, width // planes, columns)
     small_step(1)
     tail = []
     for n in range(upper):
-        sup[n] = gsum[...].astype(BF)
-        copy = send_to(sup.at[n], rup.at[n], us.at[n], ur.at[n], z, hops[3 + n])
+        szb[...] = gsum[...].astype(BF)
+        copy = send_to(szb, rup.at[n], us.at[n], ur.at[n], z, hops[3 + n])
         copy.start()
-        tail.append(copy)
         copy.wait_recv()
-        gsum[...] = sup[n].astype(F32) + rup[n].astype(F32)
+        gsum[...] = szb[...].astype(F32) + rup[n].astype(F32)
+        copy.wait_send()
     szb[...] = gsum[...].astype(BF)
     for j in range(1, planes):
         zt = lax.rem(z + j, planes)
         copy = send_to(szb.at[zt], rzb.at[j - 1], zs.at[j - 1], zr.at[j - 1], zt, i)
         copy.start()
         tail.append(copy)
+    for p in range(planes):
+        ship(p, 1)
     small_step(2)
 
     def y_finish(step, carry):
@@ -879,10 +861,10 @@
 
     y_own.wait()
     lax.fori_loop(1, chips, y_finish, 0)
-    fetch = pltpu.make_async_copy(yland, ycol, yl.at[1])
+    fetch = pltpu.make_async_copy(yland, landed_rows, yl.at[1])
     fetch.start()
     fetch.wait()
-    y_all = ycol[...]
+    y_all = landed_rows[...]
     mixed = gates[0] * dot(place[0], y_all, NN) + gates[1] * dot(place[1], y_all, NN)
     block_out[...] = (resid[...] + mixed).astype(BF)
 
@@ -924,7 +906,7 @@
     landed(px + flip, 4)
     landed(py + flip, 5)
     landed(pd + flip, 6)
-    for copy in tail + small_copies:
+    for copy in tail + small_copies[-2:]:
         copy.wait_send()
     def d_sent(target, carry):
         pl.when(spot != target)(d_copy(target).wait_send)
@@ -934,61 +916,74 @@
 
     @pl.when(host)
     def _():
-        pair_i.wait_send()
-        pair_o.wait_send()
+        for copy in pair[0] + pair[1]:
+            copy.wait_send()
 
     for is_far, copy in shipments:
         pl.when(is_far)(copy.wait_send)
 
-
-def back(planes, experts, nrouter, tokens, cot, aux, ga, act_two, q, k, v, resid,
-         probs, wd, pk, dx, dg, ysend, gi, go):
+    def dx_sent(step, carry):
+        target = lax.rem(at.me + step, at.chips)
+        for copy in copies(lax.div(target, per_plane), lax.rem(target, per_plane)):
+            copy.wait_send()
+        return carry
+
+    lax.fori_loop(1, at.chips, dx_sent, 0)
+
+
+def rear(planes, experts, nrouter, x, do, gate, tokens, cot, aux, act_two, q, k, v, resid, probs, wd, pk,
+         win, wout, ga):
     rows, width = tokens.shape
-    chips, padded, _ = ysend.shape
-    ff = gi.shape[1]
+    chips, padded, _ = x.shape
+    slots = chips * padded
+    ff = win.shape[1]
+    pieces, blocks = (1, 4) if experts <= 8 else (2, 8)
+    ga_groups = ff // width
     share, fshare, half = width // planes, ff // planes, width // 2
     upper = max(experts.bit_length() - 4, 1)
     nbits = experts.bit_length() - 1 + planes.bit_length() - 1
-    gi = gi.reshape(planes, 2, share // 2, ff)
-    go = go.reshape(planes, 2, fshare // 2, width)
     dma = pltpu.SemaphoreType.DMA
     vm = pltpu.VMEM
     sds = jax.ShapeDtypeStruct
     return pl.pallas_call(
-        functools.partial(back_kernel, planes, experts, padded, nrouter),
+        functools.partial(rear_kernel, planes, experts, padded, pieces, blocks, ga_groups, nrouter),
         out_shape=(
             sds((rows, width), BF),
             sds((rows, width), BF),
-                    sds((8, share, half), BF),
+            sds((8, share, half), BF),
             sds((nrouter + 16, width), F32),
             sds((2, share // 2, ff), BF),
             sds((2, fshare // 2, width), BF),
-            sds((chips * padded, width), BF),
+            sds((slots, width), BF),
+            sds((slots, width), BF),
         ),
-        in_specs=[vmem_spec()] * 15 + [any_spec()] * 2,
-        out_specs=(vmem_spec(),) * 6 + (any_spec(),),
+        in_specs=[vmem_spec()] * 14 + [any_spec()] * 3,
+        out_specs=(vmem_spec(),) * 6 + (any_spec(),) * 2,
         scratch_shapes=[
+            vm((width, ff), BF),
+            vm((ff, width), BF),
+            vm((slots, width), BF),
+            vm((slots, ff), BF),
+            vm((slots, ff), BF),
+            vm((chips, padded, width), BF),
+            vm((chips, 1, 128), F32),
+            vm((chips, 1, 128), F32),
+            vm((chips, padded, width), BF),
+            vm((slots, width), BF),
             vm((8, rows, half), BF),
             vm((8, rows, half), BF),
-            vm((chips * padded, width), BF),
             vm((rows, width), F32),
-            vm((rows, width), BF),
-            vm((rows, width), BF),
-            vm((rows, width), BF),
-            vm((rows, width), BF),
             vm((planes, share, half), F32),
             vm((planes, share, half), BF),
             vm((planes - 1, share, half), BF),
-            vm((upper, planes, share, half), BF),
-            vm((upper, planes, share, half), BF),
-            vm((nbits, nrouter + 16, width), F32),
+            vm((upper, planes, share, half) if experts > 8 else (1, 8, 128), BF),
+            vm((2, nrouter + 16, width), F32),
             vm((nbits, nrouter + 16, width), F32),
             vm((nrouter + 16, width), F32),
             vm((planes, share // 2, ff), BF),
-            vm((planes, share // 2, ff), BF),
             vm((planes, fshare // 2, width), BF),
-            vm((planes, fshare // 2, width), BF),
-            dma((2,)), dma((2,)), dma((2,)),
+            dma((2,)), dma((2, chips)), dma((2, chips)), dma((2,)), dma((ga_groups,)),
+            dma((2, planes)), dma((2, planes)),
             dma((planes, 2)), dma((2, 2)),
             dma((chips,)), dma((chips,)), dma((2,)),
             dma((8,)), dma((8,)),
@@ -997,10 +992,11 @@
             dma((7,)), dma((7,)), dma((nbits,)), dma((nbits,)),
         ],
         compiler_params=pltpu.CompilerParams(
-            collective_id=3, has_side_effects=True, vmem_limit_bytes=VMEM_LIMIT
+            collective_id=2, has_side_effects=True, vmem_limit_bytes=REAR_LIMIT
         ),
-        name="back",
-    )(tokens, cot, aux, ga, act_two, q, k, v, resid, probs, wd, pk, dx, dg, ysend, gi, go)
+        name="rear",
+    )(x.reshape(slots, width), do.reshape(slots, width), gate, tokens, cot, aux, act_two, q, k, v,
+      resid, probs, wd, pk, win, wout, ga.reshape(8 * rows, width))
 
 
 def finish_kernel(planes, nrouter, block_out, grad_tokens, fb, small, wi, wo,
@@ -1074,12 +1070,9 @@
         w_router, (ln1_gain, ln1_bias, ln2_gain, ln2_bias),
         w_query, w_key, w_value, w_output, frozen_in, frozen_out, new_in, new_out,
     )
-    y_rows, grad_in, grad_out, dx_back, dg_back = mid(
-        planes, experts, x_recv, do_recv, g_recv, win, wout
-    )
-    block_out, grad_tokens, dense, small, low_in, low_out, _ = back(
-        planes, experts, expert_count, tokens, cotangent, aux, ga, act_two, q, k, v,
-        resid, probs, wd, pk, dx_back, dg_back, y_rows, grad_in, grad_out,
+    block_out, grad_tokens, dense, small, low_in, low_out, _, _ = rear(
+        planes, experts, expert_count, x_recv, do_recv, g_recv, tokens, cotangent, aux, act_two, q, k, v,
+        resid, probs, wd, pk, win, wout, ga,
     )
     block_out, grad_tokens, oq, ok, ov, ow, router, norms, ogi, ogo = finish(
         planes, expert_count, block_out, grad_tokens, dense, small, low_in, low_out

time: 330 us -> 312 us (0.945); the launches traced: 326 us -> 311 us
  Pallas kernels: 324 us -> 309 us
    pallas_call x2 -> x1, Pallas kernels: 144 us -> 130 us  [rear(): pl.pallas_call(functools.partial(rear_kernel, planes, experts, padded, pi...]
where the time goes in v2:
time: 312 us; the launch traced here: 311 us
  Pallas kernels  309 us (99%)
    pallas_call x1, Pallas kernels, front(): pl.pallas_call(functools.partial(front_kernel, planes, experts, capacity,...  174 us
    pallas_call x1, Pallas kernels, rear(): pl.pallas_call(functools.partial(rear_kernel, planes, experts, padded, pi...  130 us

profile of v2, /device:TPU:0, one launch (start us, length us, event | category | flops | bytes accessed | tf_op | source)
XLA Modules:
  0.0 311.3 jit_solution(8524691692216862035)
XLA Ops:
  0.7 173.7 %front.1 = (bf16[4,768,768]{2,1,0:T(8,128)(2,1)}, bf16[32,768]{1,0:T(8,128)(2,1)}, bf16[768,3072]{1,0:T(8,128)(2,1)}, bf16[3072,768]{1,0:T(8,128)(2,1)}, bf16[25...) custom-call(bf16[256,768]{1,0:T(8,128)(2,1)} %tokens.3, ...), custom_call_target="tpu_custom_call" | custom-call | tf_op jit(solution)/shard_map/front/pallas_call | solution.py:454
  174.3 130.1 %rear.1 = (bf16[256,768]{1,0:T(8,128)(2,1)}, bf16[256,768]{1,0:T(8,128)(2,1)}, bf16[8,192,384]{2,1,0:T(8,128)(2,1)}, f32[32,768]{1,0:T(8,128)}, bf16[2,96,3072]{...) custom-call(bf16[640,768]{1,0:T(8,128)(2,1)} %bitcast.17, ...), custom_call_target="tpu_custom_call" | custom-call | tf_op jit(solution)/shard_map/rear/pallas_call | solution.py:948
  304.4 5.6 %finish.1 = (bf16[256,768]{1,0:T(8,128)(2,1)}, bf16[256,768]{1,0:T(8,128)(2,1)}, f32[192,768]{1,0:T(8,128)}, f32[192,768]{1,0:T(8,128)}, f32[192,768]{1,0:T(8,12...) custom-call(bf16[256,768]{1,0:T(8,128)(2,1)} %get-tuple-element.59.b, ...), custom_call_target="tpu_custom_call" | custom-call | tf_op jit(solution)/shard_map/finish/pallas_call | solution.py:1050
  310.0 1.3 fusion

commit v3 on v2

--- a/solution.py
+++ b/solution.py
@@ -126,10 +126,10 @@
 
 def front_kernel(planes, experts, capacity, padded, nrouter,
                  tokens, cot, segs, routes, router, g1, b1, g2, b2, wq, wk, wv, wo, fi, fo, ni, no,
-                 wd, pk, win, wout, act_one, act_two, q, k, v, att, resid, probs, aux, ga,
+                 owd, pk, win, wout, oact, oq, ok, ov, oresid, oprobs, aux, ga,
                  xland, dland, gland,
-                 packs, allow, xsend, esend, gsend, dstage, istage, ostage, ibf, obf,
-                 ld, zs, zr, ps, pr, gs, gr, es, er, fs, fr, ts, tr, tl, sa, ra):
+                 wd, act_one, act_two, q, k, v, att, resid, probs, packs, allow, xsend, esend, gsend, dstage, istage, ostage, ibf, obf,
+                 ld, zs, zr, ps, pr, gs, gr, es, er, fs, fr, ts, tr, tl, sa, ra, sv):
     at = Place(planes, experts)
     z, i, core = at.z, at.i, at.core
     rows, width = tokens.shape
@@ -411,6 +411,10 @@
     for n in range(chips):
         gsend[n] = table[n:n + 1]
     token_start(gsend, gland, 2)
+    kept_arrays = ((wd, owd), (act_two, oact), (q, oq), (k, ok), (v, ov), (resid, oresid), (probs, oprobs))
+    saves = [pltpu.make_async_copy(src, dst, sv.at[n]) for n, (src, dst) in enumerate(kept_arrays)]
+    for copy in saves:
+        copy.start()
 
     def hand_on(plane, which):
         blk = in_block(plane, core) if which == 0 else out_block(plane, core)
@@ -437,6 +441,8 @@
         copy.wait_send()
     for remote, far in remote_sends:
         pl.when(remote)(far.wait_send)
+    for copy in saves:
+        copy.wait()
 
 
 def front(planes, experts, capacity, padded, nrouter, tokens, cot, segment_ids, routes, router, norms,
@@ -458,7 +464,7 @@
             sds((nrouter + 16, width), BF),
             sds((width, ff), BF),
             sds((ff, width), BF),
-            flat, flat, flat, flat, flat, flat,
+            flat, flat, flat, flat,
             sds((rows, width), F32),
             sds((HEADS, rows, rows), F32),
             sds((rows, 128), F32),
@@ -468,8 +474,12 @@
             sds((chips, 1, 128), F32),
         ),
         in_specs=[vmem_spec()] * 9 + [any_spec()] * 8,
-        out_specs=(vmem_spec(), vmem_spec(), any_spec(), any_spec()) + (vmem_spec(),) * 9 + (any_spec(),) * 4,
+        out_specs=(any_spec(), vmem_spec()) + (any_spec(),) * 8 + (vmem_spec(),) + (any_spec(),) * 4,
         scratch_shapes=[
+            vm((4, width, width), BF),
+        ] + [vm((rows, width), BF)] * 6 + [
+            vm((rows, width), F32),
+            vm((HEADS, rows, rows), F32),
             vm((planes, nrouter + 16, share), BF),
             vm((rows, rows), F32),
             vm((chips, padded, width), BF),
@@ -484,7 +494,7 @@
             dma((planes - 1,)), dma((planes - 1,)), dma((planes - 1,)), dma((planes - 1,)),
             dma((planes - 1, 7)), dma((planes - 1, 7)),
             dma((2, 2, 2)), dma((planes, 2)), dma((planes, 2)), dma((planes, 2)),
-            dma((3, chips)), dma((3, chips)), dma((4,)), dma((8,)), dma((8,)),
+            dma((3, chips)), dma((3, chips)), dma((4,)), dma((8,)), dma((8,)), dma((7,)),
         ],
         compiler_params=pltpu.CompilerParams(
             collective_id=0, has_side_effects=True, vmem_limit_bytes=VMEM_LIMIT
@@ -499,13 +509,20 @@
 
 
 def rear_kernel(planes, experts, padded, pieces, blocks, ga_groups, nrouter,
-                x, do, gate, tokens, cot, aux, act_two, q, k, v, resid, probs, wd, pk, win, wout, ga,
+                x, do, gate, *refs):
+    back_in, refs = refs[:11], refs[11:]
+    (win, wout, ga,
                 block_out, grad_tokens, fb, osmall, wi, wo, yland, dxland,
+                tokens, cot, aux, act_two, q, k, v, resid, probs, wd, pk,
                 hwi, hwo, dy, hid, dpre, dxsend, dgsend, dgland, ysend, landed_rows,
                 gd, dsend, dres, gsum, szb, rzb, rup,
                 sms, smr, small, ri, ro,
                 ls, ts, tr, tl, gl,
-                es, er, hs, hr, ys, yr, yl, sd, rd, us, ur, zs, zr, gs, gr, ms, mr):
+                es, er, hs, hr, ys, yr, yl, sd, rd, us, ur, zs, zr, gs, gr, ms, mr, lb) = refs
+    back_held = (tokens, cot, aux, act_two, q, k, v, resid, probs, wd, pk)
+    back_loads = [
+        pltpu.make_async_copy(src, dst, lb.at[n]) for n, (src, dst) in enumerate(zip(back_in, back_held))
+    ]
     at = Place(planes, experts)
     z, i, core = at.z, at.i, at.core
     chips = at.chips
@@ -529,6 +546,8 @@
     diagonal = lax.broadcasted_iota(jnp.int32, (padded, 128), 1) == lax.broadcasted_iota(jnp.int32, (padded, 128), 0)
     load_i.wait()
     load_o.wait()
+    for copy in back_loads:
+        copy.start()
     met()
 
     def copies(plane, n):
@@ -665,6 +684,43 @@
     for copy in fetch_ga:
         copy.start()
 
+    owner = 2 * at.chip + ce
+    shipments = []
+
+    def ship(p, which):
+        src, dst = (part(hwi, half_i, p, core), wi.at[core]) if which == 0 else (part(hwo, half_o, p, core), wo.at[core])
+        near = jnp.logical_and(z == p, core == ce)
+        far_copy = send_to(src, dst, hs.at[p, which], hr.at[core, which], p, owner)
+        near_copy = pltpu.make_async_copy(src, dst, hr.at[core, which])
+        is_far = jnp.logical_and(host, jnp.logical_not(near))
+        pl.when(is_far)(far_copy.start)
+        pl.when(jnp.logical_and(host, near))(near_copy.start)
+        shipments.append((is_far, far_copy))
+
+    def add_pair(which, mine, theirs, size, chunk):
+        @pl.when(host)
+        def _():
+            for copy in pair[which]:
+                copy.wait_recv()
+
+            def add(n, carry):
+                low = pl.ds(pl.multiple_of(n * chunk, chunk), chunk)
+                for p in range(planes):
+                    here = pl.ds(pl.multiple_of((2 * p + core) * size + n * chunk, 16), chunk)
+                    mine[here, :] = (
+                        mine[here, :].astype(F32) + theirs[p, low, :].astype(F32)
+                    ).astype(BF)
+                return carry
+
+            lax.fori_loop(0, size // chunk, add, 0)
+
+    add_pair(0, hwi, ri, half_i, 16)
+    for p in range(planes):
+        ship(p, 0)
+    add_pair(1, hwo, ro, half_o, 64)
+    for p in (0, 3):
+        ship(p, 1)
+
     def dx_wait(step, carry):
         source = lax.rem(at.me + step, at.chips)
         rows_in = dxland.at[pl.ds(pl.multiple_of(source * padded, 8), padded), :]
@@ -678,6 +734,9 @@
     fetch_dx = pltpu.make_async_copy(dxland, landed_rows, yl.at[1])
     fetch_dx.start()
     fetch_dx.wait()
+
+    for copy in back_loads:
+        copy.wait()
 
     aux_v = aux[...]
     gates = [aux_v[:, 0:1], aux_v[:, 1:2]]
@@ -723,40 +782,6 @@
     for n in range(2):
         d_start(pairs + n)
 
-    owner = 2 * at.chip + ce
-    shipments = []
-
-    def ship(p, which):
-        src, dst = (part(hwi, half_i, p, core), wi.at[core]) if which == 0 else (part(hwo, half_o, p, core), wo.at[core])
-        near = jnp.logical_and(z == p, core == ce)
-        far_copy = send_to(src, dst, hs.at[p, which], hr.at[core, which], p, owner)
-        near_copy = pltpu.make_async_copy(src, dst, hr.at[core, which])
-        is_far = jnp.logical_and(host, jnp.logical_not(near))
-        pl.when(is_far)(far_copy.start)
-        pl.when(jnp.logical_and(host, near))(near_copy.start)
-        shipments.append((is_far, far_copy))
-
-    def add_pair(which, mine, theirs, size, chunk):
-        @pl.when(host)
-        def _():
-            for copy in pair[which]:
-                copy.wait_recv()
-
-            def add(n, carry):
-                low = pl.ds(pl.multiple_of(n * chunk, chunk), chunk)
-                for p in range(planes):
-                    here = pl.ds(pl.multiple_of((2 * p + core) * size + n * chunk, 16), chunk)
-                    mine[here, :] = (
-                        mine[here, :].astype(F32) + theirs[p, low, :].astype(F32)
-                    ).astype(BF)
-                return carry
-
-            lax.fori_loop(0, size // chunk, add, 0)
-
-    add_pair(0, hwi, ri, half_i, 16)
-    for p in range(planes):
-        ship(p, 0)
-
     lane = lax.broadcasted_iota(jnp.int32, (rows, 128), 1)
     masks = [(lane < HEAD).astype(F32).astype(BF), (lane >= HEAD).astype(F32).astype(BF)]
     score_scale = HEAD ** (-0.5)
@@ -815,7 +840,6 @@
             small_start(n + 1)
 
     small_start(0)
-    add_pair(1, hwo, ro, half_o, 64)
 
     small_step(0)
 
@@ -849,7 +873,7 @@
         copy = send_to(szb.at[zt], rzb.at[j - 1], zs.at[j - 1], zr.at[j - 1], zt, i)
         copy.start()
         tail.append(copy)
-    for p in range(planes):
+    for p in (1, 2):
         ship(p, 1)
     small_step(2)
 
@@ -931,9 +955,8 @@
     lax.fori_loop(1, at.chips, dx_sent, 0)
 
 
-def rear(planes, experts, nrouter, x, do, gate, tokens, cot, aux, act_two, q, k, v, resid, probs, wd, pk,
-         win, wout, ga):
-    rows, width = tokens.shape
+def rear(planes, experts, nrouter, x, do, gate, back_in, win, wout, ga):
+    rows, width = back_in[0].shape
     chips, padded, _ = x.shape
     slots = chips * padded
     ff = win.shape[1]
@@ -957,9 +980,9 @@
             sds((slots, width), BF),
             sds((slots, width), BF),
         ),
-        in_specs=[vmem_spec()] * 14 + [any_spec()] * 3,
-        out_specs=(vmem_spec(),) * 6 + (any_spec(),) * 2,
-        scratch_shapes=[
+        in_specs=[vmem_spec()] * 3 + [any_spec()] * 14,
+        out_specs=(vmem_spec(),) * 4 + (any_spec(),) * 4,
+        scratch_shapes=[vm(a.shape, a.dtype) for a in back_in] + [
             vm((width, ff), BF),
             vm((ff, width), BF),
             vm((slots, width), BF),
@@ -989,18 +1012,17 @@
             dma((8,)), dma((8,)),
             dma((upper,)), dma((upper,)),
             dma((planes - 1,)), dma((planes - 1,)),
-            dma((7,)), dma((7,)), dma((nbits,)), dma((nbits,)),
+            dma((7,)), dma((7,)), dma((nbits,)), dma((nbits,)), dma((11,)),
         ],
         compiler_params=pltpu.CompilerParams(
             collective_id=2, has_side_effects=True, vmem_limit_bytes=REAR_LIMIT
         ),
         name="rear",
-    )(x.reshape(slots, width), do.reshape(slots, width), gate, tokens, cot, aux, act_two, q, k, v,
-      resid, probs, wd, pk, win, wout, ga.reshape(8 * rows, width))
+    )(x.reshape(slots, width), do.reshape(slots, width), gate, *back_in, win, wout, ga.reshape(8 * rows, width))
 
 
 def finish_kernel(planes, nrouter, block_out, grad_tokens, fb, small, wi, wo,
-                  ob, ot, o0, o1, o2, o3, og, ov, ogi, ogo,
+                  ob, ot, o0, o1, o2, o3, og, v0, v1, v2, v3, ogi, ogo,
                   s0, s1, s2, s3, sg, sv, si, so, sem):
     z = lax.axis_index("dp")
     share = s0.shape[0]
@@ -1032,9 +1054,9 @@
         mine = jnp.where(z == p, small[:, p * share:(p + 1) * share], mine)
     sg[...] = mine[0:nrouter]
     write(sg, og)
-    for n in range(4):
+    for n, out in enumerate((v0, v1, v2, v3)):
         sv[n] = mine[nrouter + n:nrouter + n + 1]
-        write(sv.at[n], ov.at[n])
+        write(sv.at[n], out)
     for copy in copies:
         copy.wait()
 
@@ -1046,13 +1068,16 @@
     fshare = 2 * wo.shape[1]
     vm = pltpu.VMEM
     sds = jax.ShapeDtypeStruct
-    flat = ((share, width),) * 4 + ((nrouter, share), (4, 1, share), (share, ff), (fshare, width))
+    dense = ((share, width),) * 4 + ((nrouter, share),)
+    wide = ((share, ff), (fshare, width))
+    results = dense + ((1, share),) * 4 + wide
+    stages = dense + ((4, 1, share),) + wide
     return pl.pallas_call(
         functools.partial(finish_kernel, planes, nrouter),
-        out_shape=(sds((rows, width), BF),) * 2 + tuple(sds(shape, F32) for shape in flat),
+        out_shape=(sds((rows, width), BF),) * 2 + tuple(sds(shape, F32) for shape in results),
         in_specs=[vmem_spec()] * 6,
-        out_specs=(any_spec(),) * 10,
-        scratch_shapes=[vm(shape, F32) for shape in flat] + [pltpu.SemaphoreType.DMA((16,))],
+        out_specs=(any_spec(),) * 13,
+        scratch_shapes=[vm(shape, F32) for shape in stages] + [pltpu.SemaphoreType.DMA((16,))],
         compiler_params=pltpu.CompilerParams(vmem_limit_bytes=VMEM_LIMIT),
         name="finish",
     )(block_out, grad_tokens, fb, small, wi, wo)
@@ -1065,19 +1090,19 @@
     expert_count = w_router.shape[1]
     capacity = 5 * rows // (2 * expert_count)
     padded = -(-capacity // 8) * 8
-    (wd, pk, win, wout, _, act_two, q, k, v, _, resid, probs, aux, ga, x_recv, do_recv, g_recv) = front(
+    (wd, pk, win, wout, act_two, q, k, v, resid, probs, aux, ga, x_recv, do_recv, g_recv) = front(
         planes, experts, capacity, padded, expert_count, tokens, cotangent, segment_ids, routes,
         w_router, (ln1_gain, ln1_bias, ln2_gain, ln2_bias),
         w_query, w_key, w_value, w_output, frozen_in, frozen_out, new_in, new_out,
     )
     block_out, grad_tokens, dense, small, low_in, low_out, _, _ = rear(
-        planes, experts, expert_count, x_recv, do_recv, g_recv, tokens, cotangent, aux, act_two, q, k, v,
-        resid, probs, wd, pk, win, wout, ga,
+        planes, experts, expert_count, x_recv, do_recv, g_recv,
+        (tokens, cotangent, aux, act_two, q, k, v, resid, probs, wd, pk), win, wout, ga,
     )
-    block_out, grad_tokens, oq, ok, ov, ow, router, norms, ogi, ogo = finish(
+    block_out, grad_tokens, oq, ok, ov, ow, router, *norms, ogi, ogo = finish(
         planes, expert_count, block_out, grad_tokens, dense, small, low_in, low_out
     )
-    norms = norms.reshape(4, width // planes)
+    norms = [norm.reshape(width // planes) for norm in norms]
     return (
         block_out, grad_tokens, oq, ok, ov, ow, router.T,
         norms[0], norms[1], norms[2], norms[3], ogi[None], ogo[None],

time: 312 us -> 303 us (0.971)
  Pallas kernels: 309 us -> 302 us
    pallas_call x1, Pallas kernels: 130 us -> 126 us  [rear(): pl.pallas_call(functools.partial(rear_kernel, planes, experts, padded, pi...]
    pallas_call x1, Pallas kernels: 174 us -> 170 us  [front(): pl.pallas_call(functools.partial(front_kernel, planes, experts, capacity,...]
where the time goes in v3:
time: 303 us
  Pallas kernels  302 us (100%)
    pallas_call x1, Pallas kernels, front(): pl.pallas_call(functools.partial(front_kernel, planes, experts, capacity,...  170 us
    pallas_call x1, Pallas kernels, rear(): pl.pallas_call(functools.partial(rear_kernel, planes, experts, padded, pi...  126 us

profile of v3, /device:TPU:0, one launch (start us, length us, event | category | flops | bytes accessed | tf_op | source)
XLA Modules:
  0.0 302.9 jit_solution(13589333909375099637)
XLA Ops:
  0.7 170.3 %front.1 = (bf16[4,768,768]{2,1,0:T(8,128)(2,1)}, bf16[32,768]{1,0:T(8,128)(2,1)}, bf16[768,3072]{1,0:T(8,128)(2,1)}, bf16[3072,768]{1,0:T(8,128)(2,1)}, bf16[25...) custom-call(bf16[256,768]{1,0:T(8,128)(2,1)} %refs_0_.1, ...), custom_call_target="tpu_custom_call" | custom-call | tf_op jit(solution)/shard_map/front/pallas_call | solution.py:460
  170.9 126.2 %rear.1 = (bf16[256,768]{1,0:T(8,128)(2,1)}, bf16[256,768]{1,0:T(8,128)(2,1)}, bf16[8,192,384]{2,1,0:T(8,128)(2,1)}, f32[32,768]{1,0:T(8,128)}, bf16[2,96,3072]{...) custom-call(bf16[640,768]{1,0:T(8,128)(2,1)} %bitcast.17, ...), custom_call_target="tpu_custom_call" | custom-call | tf_op jit(solution)/shard_map/rear/pallas_call | solution.py:971
  297.1 5.6 %finish.1 = (bf16[256,768]{1,0:T(8,128)(2,1)}, bf16[256,768]{1,0:T(8,128)(2,1)}, f32[192,768]{1,0:T(8,128)}, f32[192,768]{1,0:T(8,128)}, f32[192,768]{1,0:T(8,12...) custom-call(bf16[256,768]{1,0:T(8,128)(2,1)} %get-tuple-element.62.b, ...), custom_call_target="tpu_custom_call" | custom-call | tf_op jit(solution)/shard_map/finish/pallas_call | solution.py:1075

commit v4 on v3

--- a/solution.py
+++ b/solution.py
@@ -129,7 +129,7 @@
                  owd, pk, win, wout, oact, oq, ok, ov, oresid, oprobs, aux, ga,
                  xland, dland, gland,
                  wd, act_one, act_two, q, k, v, att, resid, probs, packs, allow, xsend, esend, gsend, dstage, istage, ostage, ibf, obf,
-                 ld, zs, zr, ps, pr, gs, gr, es, er, fs, fr, ts, tr, tl, sa, ra, sv):
+                 ld, zs, zr, ps, pr, gs, gr, es, er, fs, fr, ts, tr, tl, sa, ra, sv, zf):
     at = Place(planes, experts)
     z, i, core = at.z, at.i, at.core
     rows, width = tokens.shape
@@ -178,13 +178,14 @@
     rqs = 2 * at.yb + 1 - core
     rqys = 2 * (1 - at.yb) + 1 - core
     xb, xo = at.xb, 1 - at.xb
-    started = []
+    started, remote_sends = [], []
     for j in range(1, planes):
         zt = lax.rem(z + j, planes)
         mine = block(z, rq, xb)
         copy = send_to(mine, mine, zs.at[j - 1], zr.at[j - 1], zt, i)
-        copy.start()
-        started.append(copy)
+        direct = jnp.logical_or(lax.div(zt, 2) == lax.div(z, 2), jnp.logical_and(zt >= 1, zt <= 2))
+        pl.when(direct)(copy.start)
+        remote_sends.append((direct, copy))
         copy = send_to(packs.at[z], packs.at[z], ps.at[j - 1], pr.at[j - 1], zt, i)
         copy.start()
         started.append(copy)
@@ -206,7 +207,6 @@
     def out_block(plane, h):
         return wout.at[pl.ds(pl.multiple_of(plane * oshare + h * ohalf, 16), ohalf), :]
 
-    remote_sends = []
 
     def ship(kind, h, which):
         zh = 3 * core if kind == 0 else 1 + core
@@ -223,11 +223,30 @@
         pl.when(jnp.logical_not(remote))(near.start)
         remote_sends.append((remote, far))
 
-    for n, kind in ((4, 0), (5, 1)):
-        loads[n].wait()
+    def ship_in(kind):
+        loads[4 + kind].wait()
         cast(istage, ibf, kind, 16)
         for h in range(2):
             ship(kind, h, 0)
+
+    ship_in(1)
+    end = 3 * (z - 1)
+    handed = []
+    for j in range(1, planes):
+        zz = lax.rem(z + planes - j, planes)
+        hand = jnp.logical_and(lax.div(zz, 2) != lax.div(z, 2), jnp.logical_and(z >= 1, z <= 2))
+        mine = block(zz, rq, xb)
+        there = lax.rem(end + planes - zz, planes)
+        copy = send_to(mine, mine, zf.at[j - 1], zr.at[jnp.maximum(there, 1) - 1], jnp.clip(end, 0, planes - 1), i)
+
+        @pl.when(hand)
+        def _():
+            send_to(mine, mine, zs.at[j - 1], zr.at[j - 1], z, i).wait_recv()
+            copy.start()
+
+        handed.append(hand)
+        remote_sends.append((hand, copy))
+    ship_in(0)
 
     shift = experts.bit_length() - 1
     above = lax.broadcasted_iota(jnp.int32, (rows, rows), 0)
@@ -308,7 +327,8 @@
     for j in range(1, planes):
         zz = lax.rem(z + planes - j, planes)
         mine = block(zz, rq, xb)
-        send_to(mine, mine, zs.at[j - 1], zr.at[j - 1], z, i).wait_recv()
+        arrival = send_to(mine, mine, zs.at[j - 1], zr.at[j - 1], z, i)
+        pl.when(jnp.logical_not(handed[j - 1]))(arrival.wait_recv)
         pass_on(mine, j, 0, at.xn)
         pass_on(mine, j, 1, at.yn)
         pass_on(mine, j, 2, at.sib)
@@ -494,7 +514,7 @@
             dma((planes - 1,)), dma((planes - 1,)), dma((planes - 1,)), dma((planes - 1,)),
             dma((planes - 1, 7)), dma((planes - 1, 7)),
             dma((2, 2, 2)), dma((planes, 2)), dma((planes, 2)), dma((planes, 2)),
-            dma((3, chips)), dma((3, chips)), dma((4,)), dma((8,)), dma((8,)), dma((7,)),
+            dma((3, chips)), dma((3, chips)), dma((4,)), dma((8,)), dma((8,)), dma((7,)), dma((planes - 1,)),
         ],
         compiler_params=pltpu.CompilerParams(
             collective_id=0, has_side_effects=True, vmem_limit_bytes=VMEM_LIMIT
@@ -868,11 +888,32 @@
         gsum[...] = szb[...].astype(F32) + rup[n].astype(F32)
         copy.wait_send()
     szb[...] = gsum[...].astype(BF)
-    for j in range(1, planes):
-        zt = lax.rem(z + j, planes)
-        copy = send_to(szb.at[zt], rzb.at[j - 1], zs.at[j - 1], zr.at[j - 1], zt, i)
-        copy.start()
-        tail.append(copy)
+    partner = z + 1 - 2 * lax.rem(z, 2)
+    others = 2 - 2 * lax.div(z, 2)
+    outer = jnp.logical_not(host)
+    copy = send_to(szb.at[partner], rzb.at[0], zs.at[0], zr.at[0], partner, i)
+    copy.start()
+    tail.append(copy)
+    inward = [
+        send_to(szb.at[others + n], rzb.at[2 + n], zs.at[1 + n], zr.at[2 + n], partner, i) for n in range(2)
+    ]
+    across = [
+        send_to(szb.at[others + n], rzb.at[1], zs.at[1 + n], zr.at[1], others + n, i) for n in range(2)
+    ]
+
+    @pl.when(outer)
+    def _():
+        for copy in inward:
+            copy.start()
+
+    @pl.when(host)
+    def _():
+        for n in range(2):
+            inward[n].wait_recv()
+            szb[others + n] = (gsum[others + n] + rzb[2 + n].astype(F32)).astype(BF)
+            across[n].start()
+
+    shipments += [(outer, copy) for copy in inward] + [(host, copy) for copy in across]
     for p in (1, 2):
         ship(p, 1)
     small_step(2)
@@ -893,9 +934,9 @@
     block_out[...] = (resid[...] + mixed).astype(BF)
 
     fin = gsum[z]
-    for j in range(1, planes):
-        send_to(rzb.at[j - 1], rzb.at[j - 1], zs.at[j - 1], zr.at[j - 1], z, i).wait_recv()
-        fin = fin + rzb[j - 1].astype(F32)
+    for n in range(2):
+        send_to(rzb.at[n], rzb.at[n], zs.at[n], zr.at[n], z, i).wait_recv()
+        fin = fin + rzb[n].astype(F32)
     fb[spot] = fin.astype(BF)
     px, py = spot + 2 - 4 * at.xb, spot + 4 - 8 * at.yb
     pd = px + 4 - 8 * at.yb
@@ -998,7 +1039,7 @@
             vm((rows, width), F32),
             vm((planes, share, half), F32),
             vm((planes, share, half), BF),
-            vm((planes - 1, share, half), BF),
+            vm((4, share, half), BF),
             vm((upper, planes, share, half) if experts > 8 else (1, 8, 128), BF),
             vm((2, nrouter + 16, width), F32),
             vm((nbits, nrouter + 16, width), F32),
@@ -1011,7 +1052,7 @@
             dma((chips,)), dma((chips,)), dma((2,)),
             dma((8,)), dma((8,)),
             dma((upper,)), dma((upper,)),
-            dma((planes - 1,)), dma((planes - 1,)),
+            dma((3,)), dma((4,)),
             dma((7,)), dma((7,)), dma((nbits,)), dma((nbits,)), dma((11,)),
         ],
         compiler_params=pltpu.CompilerParams(

time: 303 us -> 292 us (0.964)
  Pallas kernels: 302 us -> 291 us
    pallas_call x1, Pallas kernels: 170 us -> 164 us  [front(): pl.pallas_call(functools.partial(front_kernel, planes, experts, capacity,...]
    pallas_call x1, Pallas kernels: 126 us -> 121 us  [rear(): pl.pallas_call(functools.partial(rear_kernel, planes, experts, padded, pi...]
where the time goes in v4:
time: 292 us; the launch traced here: 291 us
  Pallas kernels  291 us (100%)
    pallas_call x1, Pallas kernels, front(): pl.pallas_call(functools.partial(front_kernel, planes, experts, capacity,...  164 us
    pallas_call x1, Pallas kernels, rear(): pl.pallas_call(functools.partial(rear_kernel, planes, experts, padded, pi...  121 us

profile of v4, /device:TPU:0, one launch (start us, length us, event | category | flops | bytes accessed | tf_op | source)
XLA Modules:
  0.0 291.4 jit_solution(5375679426564920327)
XLA Ops:
  0.7 163.9 %front.1 = (bf16[4,768,768]{2,1,0:T(8,128)(2,1)}, bf16[32,768]{1,0:T(8,128)(2,1)}, bf16[768,3072]{1,0:T(8,128)(2,1)}, bf16[3072,768]{1,0:T(8,128)(2,1)}, bf16[25...) custom-call(bf16[256,768]{1,0:T(8,128)(2,1)} %refs_0_.1, ...), custom_call_target="tpu_custom_call" | custom-call | tf_op jit(solution)/shard_map/front/pallas_call | solution.py:480
  164.5 121.1 %rear.1 = (bf16[256,768]{1,0:T(8,128)(2,1)}, bf16[256,768]{1,0:T(8,128)(2,1)}, bf16[8,192,384]{2,1,0:T(8,128)(2,1)}, f32[32,768]{1,0:T(8,128)}, bf16[2,96,3072]{...) custom-call(bf16[640,768]{1,0:T(8,128)(2,1)} %bitcast.17, ...), custom_call_target="tpu_custom_call" | custom-call | tf_op jit(solution)/shard_map/rear/pallas_call | solution.py:1012
  285.7 5.6 %finish.1 = (bf16[256,768]{1,0:T(8,128)(2,1)}, bf16[256,768]{1,0:T(8,128)(2,1)}, f32[192,768]{1,0:T(8,128)}, f32[192,768]{1,0:T(8,128)}, f32[192,768]{1,0:T(8,12...) custom-call(bf16[256,768]{1,0:T(8,128)(2,1)} %get-tuple-element.62.b, ...), custom_call_target="tpu_custom_call" | custom-call | tf_op jit(solution)/shard_map/finish/pallas_call | solution.py:1116

commit v5 on v4

--- a/solution.py
+++ b/solution.py
@@ -565,10 +565,6 @@
     met = greet(at)
     diagonal = lax.broadcasted_iota(jnp.int32, (padded, 128), 1) == lax.broadcasted_iota(jnp.int32, (padded, 128), 0)
     load_i.wait()
-    load_o.wait()
-    for copy in back_loads:
-        copy.start()
-    met()
 
     def copies(plane, n):
         target = plane * per_plane + n
@@ -586,7 +582,7 @@
             pltpu.make_async_copy(dgsend.at[at.me], dgland.at[at.me], tl.at[1]),
         ]
 
-    def work(plane, piece):
+    def work(plane, piece, opening=None):
         first = plane * per_plane + piece * batch
         span = pl.ds(pl.multiple_of((plane * pieces + piece) * chunk, 16), chunk)
         x_c = x[span, :]
@@ -605,6 +601,12 @@
         for b in range(blocks):
             cols = slice(b * wide, (b + 1) * wide)
             u = dot(x_c, hwi[:, cols], NN)
+            if b == 0 and opening is not None:
+                @pl.when(opening)
+                def _():
+                    load_o.wait()
+                    for copy in back_loads:
+                        copy.start()
             dz = dot(dy_c, hwo[cols, :], NT)
             square = u * u
             bent = jnp.tanh(GELU_SCALE * (u + GELU_CUBE * (square * u)))
@@ -633,7 +635,8 @@
     def remote_turn(turn, carry):
         plane = far_plane(lax.div(turn, pieces))
         piece = lax.rem(turn, pieces)
-        work(plane, piece)
+        work(plane, piece, turn == 0)
+        pl.when(turn == 0)(met)
         for n in range(batch):
             for copy in copies(plane, piece * batch + n):
                 copy.start()

time: 292 us -> 287 us (0.983)
  Pallas kernels: 291 us -> 286 us
    pallas_call x1, Pallas kernels: 121 us -> 117 us  [rear(): pl.pallas_call(functools.partial(rear_kernel, planes, experts, padded, pi...]
where the time goes in v5:
time: 287 us
  Pallas kernels  286 us (100%)
    pallas_call x1, Pallas kernels, front(): pl.pallas_call(functools.partial(front_kernel, planes, experts, capacity,...  164 us
    pallas_call x1, Pallas kernels, rear(): pl.pallas_call(functools.partial(rear_kernel, planes, experts, padded, pi...  117 us

profile of v5, /device:TPU:0, one launch (start us, length us, event | category | flops | bytes accessed | tf_op | source)
XLA Modules:
  0.0 286.9 jit_solution(10609178847972812973)
XLA Ops:
  0.7 163.9 %front.1 = (bf16[4,768,768]{2,1,0:T(8,128)(2,1)}, bf16[32,768]{1,0:T(8,128)(2,1)}, bf16[768,3072]{1,0:T(8,128)(2,1)}, bf16[3072,768]{1,0:T(8,128)(2,1)}, bf16[25...) custom-call(bf16[256,768]{1,0:T(8,128)(2,1)} %refs_0_.1, ...), custom_call_target="tpu_custom_call" | custom-call | tf_op jit(solution)/shard_map/front/pallas_call | solution.py:480
  164.5 116.5 %rear.1 = (bf16[256,768]{1,0:T(8,128)(2,1)}, bf16[256,768]{1,0:T(8,128)(2,1)}, bf16[8,192,384]{2,1,0:T(8,128)(2,1)}, f32[32,768]{1,0:T(8,128)}, bf16[2,96,3072]{...) custom-call(bf16[640,768]{1,0:T(8,128)(2,1)} %bitcast.17, ...), custom_call_target="tpu_custom_call" | custom-call | tf_op jit(solution)/shard_map/rear/pallas_call | solution.py:1015
  281.1 5.6 %finish.1 = (bf16[256,768]{1,0:T(8,128)(2,1)}, bf16[256,768]{1,0:T(8,128)(2,1)}, f32[192,768]{1,0:T(8,128)}, f32[192,768]{1,0:T(8,128)}, f32[192,768]{1,0:T(8,12...) custom-call(bf16[256,768]{1,0:T(8,128)(2,1)} %get-tuple-element.62.b, ...), custom_call_target="tpu_custom_call" | custom-call | tf_op jit(solution)/shard_map/finish/pallas_call | solution.py:1119

commit v6 on v5

--- a/solution.py
+++ b/solution.py
@@ -529,11 +529,11 @@
 
 
 def rear_kernel(planes, experts, padded, pieces, blocks, ga_groups, nrouter,
-                x, do, gate, *refs):
+                far_x, far_do, gate, *refs):
     back_in, refs = refs[:11], refs[11:]
     (win, wout, ga,
                 block_out, grad_tokens, fb, osmall, wi, wo, yland, dxland,
-                tokens, cot, aux, act_two, q, k, v, resid, probs, wd, pk,
+                x, do, tokens, cot, aux, act_two, q, k, v, resid, probs, wd, pk,
                 hwi, hwo, dy, hid, dpre, dxsend, dgsend, dgland, ysend, landed_rows,
                 gd, dsend, dres, gsum, szb, rzb, rup,
                 sms, smr, small, ri, ro,
@@ -560,11 +560,13 @@
     wide = ff // blocks
     load_i = pltpu.make_async_copy(win, hwi, ls.at[0])
     load_o = pltpu.make_async_copy(wout, hwo, ls.at[1])
-    load_i.start()
-    load_o.start()
+    load_x = [pltpu.make_async_copy(far_x, x, ls.at[2]), pltpu.make_async_copy(far_do, do, ls.at[3])]
+    for copy in load_x + [load_i, load_o]:
+        copy.start()
     met = greet(at)
     diagonal = lax.broadcasted_iota(jnp.int32, (padded, 128), 1) == lax.broadcasted_iota(jnp.int32, (padded, 128), 0)
-    load_i.wait()
+    for copy in load_x + [load_i]:
+        copy.wait()
 
     def copies(plane, n):
         target = plane * per_plane + n
@@ -1024,9 +1026,9 @@
             sds((slots, width), BF),
             sds((slots, width), BF),
         ),
-        in_specs=[vmem_spec()] * 3 + [any_spec()] * 14,
+        in_specs=[any_spec()] * 2 + [vmem_spec()] + [any_spec()] * 14,
         out_specs=(vmem_spec(),) * 4 + (any_spec(),) * 4,
-        scratch_shapes=[vm(a.shape, a.dtype) for a in back_in] + [
+        scratch_shapes=[vm((slots, width), BF)] * 2 + [vm(a.shape, a.dtype) for a in back_in] + [
             vm((width, ff), BF),
             vm((ff, width), BF),
             vm((slots, width), BF),
@@ -1049,7 +1051,7 @@
             vm((nrouter + 16, width), F32),
             vm((planes, share // 2, ff), BF),
             vm((planes, fshare // 2, width), BF),
-            dma((2,)), dma((2, chips)), dma((2, chips)), dma((2,)), dma((ga_groups,)),
+            dma((4,)), dma((2, chips)), dma((2, chips)), dma((2,)), dma((ga_groups,)),
             dma((2, planes)), dma((2, planes)),
             dma((planes, 2)), dma((2, 2)),
             dma((chips,)), dma((chips,)), dma((2,)),
@@ -1065,9 +1067,14 @@
     )(x.reshape(slots, width), do.reshape(slots, width), gate, *back_in, win, wout, ga.reshape(8 * rows, width))
 
 
-def finish_kernel(planes, nrouter, block_out, grad_tokens, fb, small, wi, wo,
-                  ob, ot, o0, o1, o2, o3, og, v0, v1, v2, v3, ogi, ogo,
-                  s0, s1, s2, s3, sg, sv, si, so, sem):
+def finish_kernel(planes, nrouter, *refs):
+    given, refs = refs[:6], refs[6:]
+    (ob, ot, o0, o1, o2, o3, og, v0, v1, v2, v3, ogi, ogo,
+     s0, s1, s2, s3, sg, sv, si, so, block_out, grad_tokens, fb, small, wi, wo, sem, lsem) = refs
+    held = (block_out, grad_tokens, fb, small, wi, wo)
+    loads = [pltpu.make_async_copy(src, dst, lsem.at[n]) for n, (src, dst) in enumerate(zip(given, held))]
+    for n in (4, 5, 2, 0, 1, 3):
+        loads[n].start()
     z = lax.axis_index("dp")
     share = s0.shape[0]
     pairs = s0.shape[1] // 128
@@ -1079,13 +1086,16 @@
         copy.start()
         copies.append(copy)
 
-    write(block_out, ob)
-    write(grad_tokens, ot)
-    for wide, low, out in ((si, wi, ogi), (so, wo, ogo)):
+    for n, (wide, low, out) in ((4, (si, wi, ogi)), (5, (so, wo, ogo))):
+        loads[n].wait()
         chunk = low.shape[1]
         for h in range(2):
             wide[h * chunk:(h + 1) * chunk, :] = low[h].astype(F32)
             write(wide.at[pl.ds(h * chunk, chunk), :], out.at[pl.ds(h * chunk, chunk), :])
+    for n, source, out in ((0, block_out, ob), (1, grad_tokens, ot)):
+        loads[n].wait()
+        write(source, out)
+    loads[2].wait()
     for m, (stage, out) in enumerate(((s0, o0), (s1, o1), (s2, o2))):
         for n in range(pairs):
             stage[:, n * 128:(n + 1) * 128] = fb[n, :, m * 128:(m + 1) * 128].astype(F32)
@@ -1093,6 +1103,7 @@
     for n in range(2):
         s3[:, n * half:(n + 1) * half] = fb[pairs + n].astype(F32)
     write(s3, o3)
+    loads[3].wait()
     mine = small[:, 0:share]
     for p in range(1, planes):
         mine = jnp.where(z == p, small[:, p * share:(p + 1) * share], mine)
@@ -1119,9 +1130,11 @@
     return pl.pallas_call(
         functools.partial(finish_kernel, planes, nrouter),
         out_shape=(sds((rows, width), BF),) * 2 + tuple(sds(shape, F32) for shape in results),
-        in_specs=[vmem_spec()] * 6,
+        in_specs=[any_spec()] * 6,
         out_specs=(any_spec(),) * 13,
-        scratch_shapes=[vm(shape, F32) for shape in stages] + [pltpu.SemaphoreType.DMA((16,))],
+        scratch_shapes=[vm(shape, F32) for shape in stages]
+        + [vm(a.shape, a.dtype) for a in (block_out, grad_tokens, fb, small, wi, wo)]
+        + [pltpu.SemaphoreType.DMA((16,)), pltpu.SemaphoreType.DMA((6,))],
         compiler_params=pltpu.CompilerParams(vmem_limit_bytes=VMEM_LIMIT),
         name="finish",
     )(block_out, grad_tokens, fb, small, wi, wo)

time: 287 us -> 285 us (level)
  no operation moved by 1% of the time
where the time goes in v6:
time: 285 us
  Pallas kernels  284 us (100%)
    pallas_call x1, Pallas kernels, front(): pl.pallas_call(functools.partial(front_kernel, planes, experts, capacity,...  164 us
    pallas_call x1, Pallas kernels, rear(): pl.pallas_call(functools.partial(rear_kernel, planes, experts, padded, pi...  116 us

profile of v6, /device:TPU:0, one launch (start us, length us, event | category | flops | bytes accessed | tf_op | source)
XLA Modules:
  0.0 285.2 jit_solution(11636368819478119396)
XLA Ops:
  0.7 163.9 %front.1 = (bf16[4,768,768]{2,1,0:T(8,128)(2,1)}, bf16[32,768]{1,0:T(8,128)(2,1)}, bf16[768,3072]{1,0:T(8,128)(2,1)}, bf16[3072,768]{1,0:T(8,128)(2,1)}, bf16[25...) custom-call(bf16[256,768]{1,0:T(8,128)(2,1)} %refs_0_.1, ...), custom_call_target="tpu_custom_call" | custom-call | tf_op jit(solution)/shard_map/front/pallas_call | solution.py:480
  164.5 115.7 %rear.1 = (bf16[256,768]{1,0:T(8,128)(2,1)}, bf16[256,768]{1,0:T(8,128)(2,1)}, bf16[8,192,384]{2,1,0:T(8,128)(2,1)}, f32[32,768]{1,0:T(8,128)}, bf16[2,96,3072]{...) custom-call(bf16[640,768]{1,0:T(8,128)(2,1)} %bitcast.17, ...), custom_call_target="tpu_custom_call" | custom-call | tf_op jit(solution)/shard_map/rear/pallas_call | solution.py:1017
  280.3 4.7 %finish.1 = (bf16[256,768]{1,0:T(8,128)(2,1)}, bf16[256,768]{1,0:T(8,128)(2,1)}, f32[192,768]{1,0:T(8,128)}, f32[192,768]{1,0:T(8,128)}, f32[192,768]{1,0:T(8,12...) custom-call(bf16[256,768]{1,0:T(8,128)(2,1)} %get-tuple-element.62.r, ...), custom_call_target="tpu_custom_call" | custom-call | tf_op jit(solution)/shard_map/finish/pallas_call | solution.py:1130
